TPU v7x, 256 devices: a whole 4x4x8 slice. The times are simulated.
256 devices in a mesh: tm: 8 (over x, core), rows: 32 (over y, z).
Axes of the slice: x: 4, y: 4, z: 8, core: 2. Of those that a mesh axis runs over, the one named last changes fastest.
Arguments:
- latent: bfloat16 [32, 192, 128, 128], P('tm', None, 'rows'), may hold values from -6 to 6
- clip_ids: int32 [32], replicated, may hold values from 0 to 3, as said below
- gain_in: float32 [192], replicated, may hold values from 0.1 to 1.9
- conv_in: bfloat16 [3, 3, 3, 96, 192], replicated, may hold values from -0.078125 to 0.078125
- bias_in: float32 [96], replicated, may hold values from -3 to 3
- gain_mid: float32 [96], replicated, may hold values from 0.1 to 1.9
- conv_mid: bfloat16 [3, 3, 3, 96, 96], replicated, may hold values from -0.125 to 0.125
- bias_mid: float32 [96], replicated, may hold values from -3 to 3
- skip_weight: bfloat16 [96, 192], replicated, may hold values from -0.4375 to 0.4375
- skip_bias: float32 [96], replicated, may hold values from -3 to 3
Outputs:
- decoded: bfloat16 [32, 96, 128, 128], P('tm', None, 'rows')
Inputs may be any that keep to these rules, and one draw needn't show every extreme that they name: `clip_ids`: clip number of each frame; numbers never fall along the frames and every number appears; each clip lies on consecutive frames, and every clip other than the window's first and last holds 1 + 4 k frames, at most 21.
All inputs are finite; a program needn't handle non-finite values.
Results may differ from a plain program's by a relative error of at most 0.0075.
Values may be sent and summed in bfloat16 or wider, within the bound.
A program may use at most 64 MiB of HBM per device.

v0:
```python
import jax
import jax.numpy as jnp
from jax import lax
from jax.sharding import PartitionSpec as P


def passed_along(block, axis, distance):
    devices = range(lax.axis_size(axis))
    route = [(i - distance, i) for i in devices if i - distance in devices]
    return lax.ppermute(block, axis, route)


def padded_2(shard, sides, width):
    for axis, dim in sides:
        size, length = (lax.axis_size(axis), shard.shape[dim])
        up = [(i, (i + 1) % size) for i in range(size - 1)]
        down = [(j, i) for i, j in up]
        last = lax.slice_in_dim(shard, length - width, length, axis=dim)
        first = lax.slice_in_dim(shard, 0, width, axis=dim)
        before = lax.ppermute(last, axis, up)
        after = lax.ppermute(first, axis, down)
        shard = jnp.concatenate([before, shard, after], axis=dim)
    return shard


def keep_table(clip_ids, start, count):
    frames = start + jnp.arange(count, dtype=jnp.int32)
    final_index = clip_ids.shape[0] - 1
    own_clip = jnp.take(clip_ids, jnp.clip(frames, 0, final_index))
    tables = []
    for back_step in range(3):
        source = frames - back_step
        src_clip = jnp.take(clip_ids, jnp.clip(source, 0, final_index))
        tables.append(((source >= 0) & (src_clip == own_clip)).astype(jnp.float32))
    return jnp.stack(tables)


def norm_silu(values, gain):
    floats = values.astype(jnp.float32)
    mean_sq = jnp.mean(floats * floats, axis=1, keepdims=True)
    scaled = floats * lax.rsqrt(mean_sq + 1e-06) * gain[None, :, None, None]
    return jax.nn.silu(scaled).astype(jnp.bfloat16)


def causal_conv(padded, weight, keep, out_frames):
    total = None
    for t_tap in range(3):
        slab = padded[t_tap : t_tap + out_frames]
        part = lax.conv_general_dilated(
            slab,
            weight[t_tap],
            (1, 1),
            ((0, 0), (1, 1)),
            dimension_numbers=("NCHW", "HWOI", "NCHW"),
            preferred_element_type=jnp.float32,
        )
        term = part * keep[2 - t_tap][:, None, None, None]
        total = term if total is None else total + term
    return total


def shards(
    latent,
    clip_ids,
    gain_in,
    conv_in,
    bias_in,
    gain_mid,
    conv_mid,
    bias_mid,
    skip_weight,
    skip_bias,
):
    frames_dev = latent.shape[0]
    start = lax.axis_index("tm") * frames_dev
    keep_own = keep_table(clip_ids, start, frames_dev)
    first = norm_silu(latent, gain_in)
    earlier = passed_along(first[frames_dev - 2 :], "tm", 1)
    extended = jnp.concatenate([earlier, first], axis=0)
    extended = padded_2(extended, (("rows", 2),), 1)
    hidden = causal_conv(extended, conv_in, keep_own, frames_dev)
    hidden = (hidden + bias_in[None, :, None, None]).astype(jnp.bfloat16)
    second = norm_silu(hidden, gain_mid)
    earlier_mid = passed_along(second[frames_dev - 2 :], "tm", 1)
    extended_mid = jnp.concatenate([earlier_mid, second], axis=0)
    extended_mid = padded_2(extended_mid, (("rows", 2),), 1)
    tail = causal_conv(extended_mid, conv_mid, keep_own, frames_dev)
    short = jnp.einsum("oc,fcrw->forw", skip_weight, latent, preferred_element_type=jnp.float32)
    result = tail + bias_mid[None, :, None, None] + short + skip_bias[None, :, None, None]
    return result.astype(jnp.bfloat16)


def solution(mesh):
    return jax.shard_map(
        shards,
        mesh=mesh,
        in_specs=(P("tm", None, "rows", None), P(), P(), P(), P(), P(), P(), P(), P(), P()),
        out_specs=P("tm", None, "rows", None),
        check_vma=False,
    )
```

profile of v0, /device:TPU:50, one launch (start us, length us, event | category | flops | bytes accessed | tf_op | source)
XLA Modules:
  0.0 96.8 jit_solution(1759691102827882856)
XLA Ops:
  0.0 1.3 %fusion.18 = f32[4,4,128]{2,1,0:T(4,128)S(1)} fusion(bf16[4,192,4,128]{3,2,1,0:T(4,128)(2,1)} %param.12), kind=kLoop, calls=%fused_computation.26 | loop fusion | flops 1177600 | bytes 794624 | tf_op jit(solution)/shard_map/reduce_sum | solution.py:40
  1.3 1.7 %fusion.25 = bf16[4,192,4,128]{3,1,2,0:T(8,128)(2,1)S(1)} fusion(f32[192]{0:T(256)} %param.14, f32[4,4,128]{2,1,0:T(4,128)S(1)} %add_rsqrt_fusion.1, bf16[4,192,4,128]{3,2,1,0:T(4,128)(2,1)} %param.12), kind=kLoop, calls=%fused_computation.33 | loop fusion | flops 3145728 | bytes 1581824 | tf_op jit(solution)/shard_map/convert_element_type | solution.py:42
  3.1 1.9 %collective-permute-start = (bf16[2,192,4,128]{3,1,2,0:T(8,128)(2,1)S(1)}, bf16[2,192,4,128]{3,1,2,0:T(8,128)(2,1)S(1)}, u32[]{:S(2)}, u32[]{:S(2)}) collective-permute-start(bf16[2,192,4,128]{3,1,2,0:T(8,128)(2,1)S(1)} %slice.87), channel_id=1, source_target_pairs={{0,32},{32,64},{64,96},{96,128},{128,160},{160,192},{192,224},{1,3... | collective-permute-start | bytes 1179656 | tf_op jit(solution)/shard_map/ppermute | solution.py:10
  5.0 0.6 gather_fusion.1
  5.7 0.6 gather_fusion.2
  6.4 0.6 gather_fusion
  7.0 5.2 %collective-permute-done = bf16[2,192,4,128]{3,1,2,0:T(8,128)(2,1)S(1)} collective-permute-done((bf16[2,192,4,128]{3,1,2,0:T(8,128)(2,1)S(1)}, bf16[2,192,4,128]{3,1,2,0:T(8,128)(2,1)S(1)}, u32[]{:S(2)}, u32[]{:S(2)}) %collective-permute-start) | collective-permute-done | bytes 393248 | tf_op jit(solution)/shard_map/ppermute | solution.py:10
  12.2 3.8 %collective-permute-start.1 = (bf16[6,192,1,128]{3,1,2,0:T(8,128)(2,1)S(1)}, bf16[6,192,1,128]{3,1,2,0:T(8,128)(2,1)S(1)}, u32[]{:S(2)}, u32[]{:S(2)}) collective-permute-start(bf16[6,192,1,128]{3,1,2,0:T(8,128)(2,1)S(1)} %get-tuple-element.12), channel_id=1, source_target_pairs={{0,1},{1,2},{2,3},{3,4},{4,5},{5,6},{6,7},{7,8},{8,9},{9,10},{10,1... | collective-permute-start | bytes 884744 | tf_op jit(solution)/shard_map/ppermute | solution.py:20
  16.1 2.0 %collective-permute-start.2 = (bf16[6,192,1,128]{3,1,2,0:T(8,128)(2,1)S(1)}, bf16[6,192,1,128]{3,1,2,0:T(8,128)(2,1)S(1)}, u32[]{:S(2)}, u32[]{:S(2)}) collective-permute-start(bf16[6,192,1,128]{3,1,2,0:T(8,128)(2,1)S(1)} %get-tuple-element.13), channel_id=1, source_target_pairs={{1,0},{2,1},{3,2},{4,3},{5,4},{6,5},{7,6},{8,7},{9,8},{10,9},{11,1... | collective-permute-start | bytes 884744 | tf_op jit(solution)/shard_map/ppermute | solution.py:21
  18.1 4.0 %collective-permute-done.1 = bf16[6,192,1,128]{3,1,2,0:T(8,128)(2,1)S(1)} collective-permute-done((bf16[6,192,1,128]{3,1,2,0:T(8,128)(2,1)S(1)}, bf16[6,192,1,128]{3,1,2,0:T(8,128)(2,1)S(1)}, u32[]{:S(2)}, u32[]{:S(2)}) %collective-permute-start.1) | collective-permute-done | bytes 294944 | tf_op jit(solution)/shard_map/ppermute | solution.py:20
  22.2 3.7 %collective-permute-done.2 = bf16[6,192,1,128]{3,1,2,0:T(8,128)(2,1)S(1)} collective-permute-done((bf16[6,192,1,128]{3,1,2,0:T(8,128)(2,1)S(1)}, bf16[6,192,1,128]{3,1,2,0:T(8,128)(2,1)S(1)}, u32[]{:S(2)}, u32[]{:S(2)}) %collective-permute-start.2) | collective-permute-done | bytes 294944 | tf_op jit(solution)/shard_map/ppermute | solution.py:21
  25.9 0.2 pad_maximum_fusion
  26.1 2.2 %slice_bitcast_fusion = (bf16[192,6,4,128]{3,0,1,2:T(8,128)(2,1)S(1)}, bf16[192,6,4,128]{3,0,1,2:T(8,128)(2,1)}, bf16[192,6,4,128]{3,0,1,2:T(8,128)(2,1)}) fusion(bf16[6,192,6,128]{3,1,2,0:T(8,128)(2,1)S(1)} %pad_maximum_fusion), kind=kLoop, calls=%fused_computation.59 | loop fusion | bytes 7077888 | tf_op jit(solution)/shard_map/slice | solution.py:48
  28.4 2.6 %copy.72 = bf16[192,6,4,128]{0,2,3,1:T(4,128)(2,1)S(1)} copy(bf16[192,6,4,128]{3,0,1,2:T(8,128)(2,1)} %get-tuple-element.7) | data formatting | bytes 2359296
  31.0 0.7 pad.2.clone
  31.8 1.9 %fusion.4 = bf16[192,6,4,8,19]{0,2,4,3,1:T(4,128)(2,1)} fusion(bf16[192,6,4,7,2]{0,2,4,3,1:T(4,128)(2,1)S(1)} %slice.91, bf16[192,6,4,8,17]{0,2,4,3,1:T(4,128)(2,1)S(1)} %bitcast.113), kind=kLoop, calls=%fused_computation.10 | loop fusion | flops 4202496 | bytes 2783232 | tf_op jit(solution)/shard_map/conv_general_dilated | solution.py:49
  33.7 2.6 %copy.71 = bf16[192,6,4,128]{0,2,3,1:T(4,128)(2,1)S(1)} copy(bf16[192,6,4,128]{3,0,1,2:T(8,128)(2,1)} %get-tuple-element.8) | data formatting | bytes 2359296
  36.3 0.7 pad.clone
  37.1 1.9 %fusion.3 = bf16[192,6,4,8,19]{0,2,4,3,1:T(4,128)(2,1)} fusion(bf16[192,6,4,7,2]{0,2,4,3,1:T(4,128)(2,1)S(1)} %slice.89, bf16[192,6,4,8,17]{0,2,4,3,1:T(4,128)(2,1)S(1)} %bitcast.115), kind=kLoop, calls=%fused_computation.9 | loop fusion | flops 4202496 | bytes 2783232 | tf_op jit(solution)/shard_map/conv_general_dilated | solution.py:49
  39.0 1.0 %copy.73 = bf16[192,6,4,128]{0,2,3,1:T(4,128)(2,1)S(1)} copy(bf16[192,6,4,128]{3,0,1,2:T(8,128)(2,1)S(1)} %get-tuple-element.6) | data formatting | bytes 2359296
  40.0 0.7 pad.4.clone
  40.9 1.1 %fusion.5 = bf16[192,6,4,8,19]{0,2,4,3,1:T(4,128)(2,1)S(1)} fusion(bf16[192,6,4,7,2]{0,2,4,3,1:T(4,128)(2,1)S(1)} %slice.93, bf16[192,6,4,8,17]{0,2,4,3,1:T(4,128)(2,1)S(1)} %bitcast.117), kind=kLoop, calls=%fused_computation.11 | loop fusion | flops 4202496 | bytes 2783232 | tf_op jit(solution)/shard_map/conv_general_dilated | solution.py:49
  42.0 0.2 broadcast.80
  42.2 0.1 copy-done.3
  42.3 0.4 copy-done.9
  42.7 2.9 %fusion.44 = f32[4,32,17,96]{3,1,2,0:T(8,128)S(1)} fusion(bf16[192,6,4,8,19]{0,2,4,3,1:T(4,128)(2,1)S(1)} %copy-done.3, f32[4,32,17,96]{3,0,2,1:T(4,128)S(1)} %bitcast.126, pred[32,17]{0,1:T(8,128)(4,1)S(1)} %copy-done.13, bf16[3,3,3,96,192]{4,3,2,1,0:T(8,128)(2,1)S(1)} %copy-done.9), kind=kOutput, calls=%fused_computation.48 | convolution fusion | flops 722362368 | bytes 4262912 | tf_op jit(solution)/shard_map/conv_general_dilated | solution.py:49
  45.6 0.2 broadcast.77
  45.9 3.0 %fusion.38 = f32[4,32,17,96]{3,1,2,0:T(8,128)S(1)} fusion(f32[4,32,17,96]{3,1,2,0:T(8,128)S(1)} %fusion.44, bf16[192,6,4,8,19]{0,2,4,3,1:T(4,128)(2,1)S(1)} %copy-done.4, f32[4,32,17,96]{3,0,2,1:T(4,128)S(1)} %bitcast.128, pred[32,17]{0,1:T(8,128)(4,1)S(1)} %copy-done.13, bf16[3,3,3,96,192]{4,3,2,1,0:T(8,128)(2,1)S(1)} %copy-done.9), kind=kOutput, calls=%fused_computation.46 | convolution fusion | flops 722571264 | bytes 5377024 | tf_op jit(solution)/shard_map/conv_general_dilated | solution.py:49
  48.9 0.2 broadcast.83
  49.1 3.0 %multiply_reduce_fusion = (f32[4,32,17]{1,2,0:T(8,128)S(1)}, f32[4,32,17,96]{3,1,2,0:T(8,128)S(1)}) fusion(f32[96]{0:T(128)S(1)} %copy-done.11, f32[4,32,17,96]{3,1,2,0:T(8,128)S(1)} %fusion.38, f32[4,32,17,96]{3,0,2,1:T(4,128)S(1)} %bitcast.130, bf16[3,3,3,96,192]{4,3,2,1,0:T(8,128)(2,1)S(1)} %copy-done.9, bf16[192,6,4,8,19]{0,2,4,3,1:T(4,128)(2,1)S(1)} %fusion.5, ...), kind=kOutput, calls=%fused_computation.62 | convolution fusion | flops 723613568 | bytes 5386240 | tf_op jit(solution)/shard_map/conv_general_dilated | solution.py:49
  52.1 0.7 copy.53
  52.9 0.1 copy.54
  53.0 0.1 reshape.55
  53.1 0.9 copy.55
  53.9 1.6 %fusion.70 = bf16[4,96,4,128]{1,2,3,0:T(4,128)(2,1)S(1)} fusion(f32[4,4,136,96]{3,0,2,1:T(4,128)S(1)} %bitcast.118, f32[96]{0:T(128)S(1)} %copy-done.8, f32[4,4,128]{1,2,0:T(8,128)} %copy.55), kind=kLoop, calls=%fused_computation.70 | loop fusion | flops 1376256 | bytes 1188224 | tf_op jit(solution)/shard_map/convert_element_type | solution.py:42
  55.6 0.1 slice.96
  55.7 1.9 %collective-permute-start.3 = (bf16[2,96,4,128]{1,2,3,0:T(4,128)(2,1)S(1)}, bf16[2,96,4,128]{1,2,3,0:T(4,128)(2,1)S(1)}, u32[]{:S(2)}, u32[]{:S(2)}) collective-permute-start(bf16[2,96,4,128]{1,2,3,0:T(4,128)(2,1)S(1)} %slice.96), channel_id=1, source_target_pairs={{0,32},{32,64},{64,96},{96,128},{128,160},{160,192},{192,224},{1,3... | collective-permute-start | bytes 589832 | tf_op jit(solution)/shard_map/ppermute | solution.py:10
  57.6 5.8 %collective-permute-done.3 = bf16[2,96,4,128]{1,2,3,0:T(4,128)(2,1)S(1)} collective-permute-done((bf16[2,96,4,128]{1,2,3,0:T(4,128)(2,1)S(1)}, bf16[2,96,4,128]{1,2,3,0:T(4,128)(2,1)S(1)}, u32[]{:S(2)}, u32[]{:S(2)}) %collective-permute-start.3) | collective-permute-done | bytes 196640 | tf_op jit(solution)/shard_map/ppermute | solution.py:10
  63.4 0.8 fusion.87
  64.2 5.0 %collective-permute-start.4 = (bf16[6,96,1,128]{1,2,3,0:T(2,128)(2,1)S(1)}, bf16[6,96,1,128]{1,2,3,0:T(2,128)(2,1)S(1)}, u32[]{:S(2)}, u32[]{:S(2)}) collective-permute-start(bf16[6,96,1,128]{1,2,3,0:T(2,128)(2,1)S(1)} %get-tuple-element.14), channel_id=1, source_target_pairs={{0,1},{1,2},{2,3},{3,4},{4,5},{5,6},{6,7},{7,8},{8,9},{9,10},{10,1... | collective-permute-start | bytes 442376 | tf_op jit(solution)/shard_map/ppermute | solution.py:20
  69.2 2.1 %collective-permute-start.5 = (bf16[6,96,1,128]{1,2,3,0:T(2,128)(2,1)S(1)}, bf16[6,96,1,128]{1,2,3,0:T(2,128)(2,1)S(1)}, u32[]{:S(2)}, u32[]{:S(2)}) collective-permute-start(bf16[6,96,1,128]{1,2,3,0:T(2,128)(2,1)S(1)} %get-tuple-element.15), channel_id=1, source_target_pairs={{1,0},{2,1},{3,2},{4,3},{5,4},{6,5},{7,6},{8,7},{9,8},{10,9},{11,1... | collective-permute-start | bytes 442376 | tf_op jit(solution)/shard_map/ppermute | solution.py:21
  71.4 5.2 %collective-permute-done.4 = bf16[6,96,1,128]{1,2,3,0:T(2,128)(2,1)S(1)} collective-permute-done((bf16[6,96,1,128]{1,2,3,0:T(2,128)(2,1)S(1)}, bf16[6,96,1,128]{1,2,3,0:T(2,128)(2,1)S(1)}, u32[]{:S(2)}, u32[]{:S(2)}) %collective-permute-start.4) | collective-permute-done | bytes 147488 | tf_op jit(solution)/shard_map/ppermute | solution.py:20
  76.6 5.3 %collective-permute-done.5 = bf16[6,96,1,128]{1,2,3,0:T(2,128)(2,1)S(1)} collective-permute-done((bf16[6,96,1,128]{1,2,3,0:T(2,128)(2,1)S(1)}, bf16[6,96,1,128]{1,2,3,0:T(2,128)(2,1)S(1)}, u32[]{:S(2)}, u32[]{:S(2)}) %collective-permute-start.5) | collective-permute-done | bytes 147488 | tf_op jit(solution)/shard_map/ppermute | solution.py:21
  81.9 1.6 %pad_maximum_fusion.1 = bf16[6,96,6,128]{1,2,3,0:T(8,128)(2,1)S(1)} fusion(bf16[6,96,1,128]{1,2,3,0:T(2,128)(2,1)S(1)} %collective-permute-done.5, bf16[4,96,4,128]{1,2,3,0:T(4,128)(2,1)S(1)} %fusion.70, bf16[2,96,4,128]{1,2,3,0:T(4,128)(2,1)S(1)} %collective-permute-done.3, bf16[6,96,1,128]{1,2,3,0:T(2,128)(2,1)S(1)} %collective-permute-done.4), kind=kLoop, calls=%fused_computation.34 | loop fusion | flops 3538944 | bytes 1769472 | tf_op jit(solution)/shard_map/concatenate | solution.py:22
  83.5 0.5 slice_bitcast_fusion.3
  84.1 0.6 copy.76
  84.7 0.4 pad.10.clone
  85.1 0.5 fusion.73
  85.6 0.6 copy.74
  86.3 0.4 pad.6.clone
  86.7 0.5 fusion.71
  87.2 0.6 copy.75
  87.9 0.4 pad.8.clone
  88.3 0.5 fusion.72
  88.8 0.1 copy-done.10
  88.9 1.5 %fusion.28 = f32[4,32,17,96]{3,1,2,0:T(8,128)S(1)} fusion(f32[4,32,17,96]{3,0,2,1:T(4,128)S(1)} %bitcast.127, bf16[96,6,4,8,19]{0,2,4,3,1:T(4,128)(2,1)S(1)} %fusion.72, pred[32,17]{0,1:T(8,128)(4,1)S(1)} %copy-done.13, bf16[3,3,3,96,96]{4,3,2,1,0:T(8,128)(2,1)S(1)} %copy-done.10), kind=kOutput, calls=%fused_computation.40 | convolution fusion | flops 361390080 | bytes 3107840 | tf_op jit(solution)/shard_map/conv_general_dilated | solution.py:49
  90.5 1.6 %fusion.27 = f32[4,32,17,96]{3,1,2,0:T(8,128)S(1)} fusion(f32[4,32,17,96]{3,1,2,0:T(8,128)S(1)} %fusion.28, f32[4,32,17,96]{3,0,2,1:T(4,128)S(1)} %bitcast.129, bf16[96,6,4,8,19]{0,2,4,3,1:T(4,128)(2,1)S(1)} %fusion.71, pred[32,17]{0,1:T(8,128)(4,1)S(1)} %copy-done.13, bf16[3,3,3,96,96]{4,3,2,1,0:T(8,128)(2,1)S(1)} %copy-done.10), kind=kOutput, calls=%fused_computation.39 | convolution fusion | flops 361598976 | bytes 4221952 | tf_op jit(solution)/shard_map/conv_general_dilated | solution.py:49
  92.1 1.6 %fusion.31 = f32[4,32,17,96]{3,1,2,0:T(8,128)S(1)} fusion(f32[4,32,17,96]{3,1,2,0:T(8,128)S(1)} %fusion.27, f32[4,32,17,96]{3,0,2,1:T(4,128)S(1)} %bitcast.131, bf16[96,6,4,8,19]{0,2,4,3,1:T(4,128)(2,1)S(1)} %fusion.73, f32[96]{0:T(128)S(1)} %copy-done.12, pred[32,17]{0,1:T(8,128)(4,1)S(1)} %copy-done.13, bf16[3,3,3,96,96]{4,3,2,1,0:T(8,128)(2,1)S(1)} %copy-done.10), kind=kOutput, calls=%fused_computation.43 | convolution fusion | flops 361807872 | bytes 4222464 | tf_op jit(solution)/shard_map/conv_general_dilated | solution.py:49
  93.7 0.7 copy.65
  94.5 0.1 slice.105
  94.5 0.3 copy.70
  94.9 0.7 copy-done.2
  95.6 0.3 fusion.67
  95.8 0.9 copy.68
  (42 shorter events, 0.5 us)
Async XLA Ops:
  0.0 94.9 %copy-start = (bf16[96,192]{1,0:T(8,128)(2,1)S(1)}, bf16[96,192]{1,0:T(8,128)(2,1)}, u32[]{:S(2)}) copy-start(bf16[96,192]{1,0:T(8,128)(2,1)} %param.20) | copy-start | bytes 110596
  0.0 5.0 %copy-start.1 = (s32[32]{0:T(128)S(1)}, s32[32]{0:T(128)}, u32[]{:S(2)}) copy-start(s32[32]{0:T(128)} %param.13) | copy-start | bytes 388
  3.1 9.1 %collective-permute-start = (bf16[2,192,4,128]{3,1,2,0:T(8,128)(2,1)S(1)}, bf16[2,192,4,128]{3,1,2,0:T(8,128)(2,1)S(1)}, u32[]{:S(2)}, u32[]{:S(2)}) collective-permute-start(bf16[2,192,4,128]{3,1,2,0:T(8,128)(2,1)S(1)} %slice.87), channel_id=1, source_target_pairs={{0,32},{32,64},{64,96},{96,128},{128,160},{160,192},{192,224},{1,3... | collective-permute-start | bytes 1179656 | tf_op jit(solution)/shard_map/ppermute | solution.py:10
  12.2 9.9 %collective-permute-start.1 = (bf16[6,192,1,128]{3,1,2,0:T(8,128)(2,1)S(1)}, bf16[6,192,1,128]{3,1,2,0:T(8,128)(2,1)S(1)}, u32[]{:S(2)}, u32[]{:S(2)}) collective-permute-start(bf16[6,192,1,128]{3,1,2,0:T(8,128)(2,1)S(1)} %get-tuple-element.12), channel_id=1, source_target_pairs={{0,1},{1,2},{2,3},{3,4},{4,5},{5,6},{6,7},{7,8},{8,9},{9,10},{10,1... | collective-permute-start | bytes 884744 | tf_op jit(solution)/shard_map/ppermute | solution.py:20
  16.1 9.8 %collective-permute-start.2 = (bf16[6,192,1,128]{3,1,2,0:T(8,128)(2,1)S(1)}, bf16[6,192,1,128]{3,1,2,0:T(8,128)(2,1)S(1)}, u32[]{:S(2)}, u32[]{:S(2)}) collective-permute-start(bf16[6,192,1,128]{3,1,2,0:T(8,128)(2,1)S(1)} %get-tuple-element.13), channel_id=1, source_target_pairs={{1,0},{2,1},{3,2},{4,3},{5,4},{6,5},{7,6},{8,7},{9,8},{10,9},{11,1... | collective-permute-start | bytes 884744 | tf_op jit(solution)/shard_map/ppermute | solution.py:21
  40.8 1.5 %copy-start.3 = (bf16[192,6,4,8,19]{0,2,4,3,1:T(4,128)(2,1)S(1)}, bf16[192,6,4,8,19]{0,2,4,3,1:T(4,128)(2,1)}, u32[]{:S(2)}) copy-start(bf16[192,6,4,8,19]{0,2,4,3,1:T(4,128)(2,1)} %fusion.4) | copy-start | bytes 4202500
  40.8 1.9 %copy-start.9 = (bf16[3,3,3,96,192]{4,3,2,1,0:T(8,128)(2,1)S(1)}, bf16[3,3,3,96,192]{4,3,2,1,0:T(8,128)(2,1)}, u32[]{:S(2)}) copy-start(bf16[3,3,3,96,192]{4,3,2,1,0:T(8,128)(2,1)} %param.15) | copy-start | bytes 2985988
  40.8 1.9 %copy-start.13 = (pred[32,17]{0,1:T(8,128)(4,1)S(1)}, pred[32,17]{0,1:T(8,128)(4,1)}, u32[]{:S(2)}) copy-start(pred[32,17]{0,1:T(8,128)(4,1)} %constant.70) | copy-start | bytes 1636
  42.7 3.1 %copy-start.4 = (bf16[192,6,4,8,19]{0,2,4,3,1:T(4,128)(2,1)S(1)}, bf16[192,6,4,8,19]{0,2,4,3,1:T(4,128)(2,1)}, u32[]{:S(2)}) copy-start(bf16[192,6,4,8,19]{0,2,4,3,1:T(4,128)(2,1)} %fusion.3) | copy-start | bytes 4202500
  45.9 3.2 %copy-start.11 = (f32[96]{0:T(128)S(1)}, f32[96]{0:T(128)}, u32[]{:S(2)}) copy-start(f32[96]{0:T(128)} %param.16) | copy-start | bytes 1156
  49.1 3.0 %copy-start.5 = (f32[4,4,136,96]{3,0,2,1:T(4,128)}, f32[4,4,136,96]{3,0,2,1:T(4,128)S(1)}, u32[]{:S(2)}) copy-start(f32[4,4,136,96]{3,0,2,1:T(4,128)S(1)} %broadcast.83) | copy-start | bytes 2506756
  52.1 1.8 %copy-start.8 = (f32[96]{0:T(128)S(1)}, f32[96]{0:T(128)}, u32[]{:S(2)}) copy-start(f32[96]{0:T(128)} %param.17) | copy-start | bytes 1156
  55.7 7.7 %collective-permute-start.3 = (bf16[2,96,4,128]{1,2,3,0:T(4,128)(2,1)S(1)}, bf16[2,96,4,128]{1,2,3,0:T(4,128)(2,1)S(1)}, u32[]{:S(2)}, u32[]{:S(2)}) collective-permute-start(bf16[2,96,4,128]{1,2,3,0:T(4,128)(2,1)S(1)} %slice.96), channel_id=1, source_target_pairs={{0,32},{32,64},{64,96},{96,128},{128,160},{160,192},{192,224},{1,3... | collective-permute-start | bytes 589832 | tf_op jit(solution)/shard_map/ppermute | solution.py:10
  64.2 12.4 %collective-permute-start.4 = (bf16[6,96,1,128]{1,2,3,0:T(2,128)(2,1)S(1)}, bf16[6,96,1,128]{1,2,3,0:T(2,128)(2,1)S(1)}, u32[]{:S(2)}, u32[]{:S(2)}) collective-permute-start(bf16[6,96,1,128]{1,2,3,0:T(2,128)(2,1)S(1)} %get-tuple-element.14), channel_id=1, source_target_pairs={{0,1},{1,2},{2,3},{3,4},{4,5},{5,6},{6,7},{7,8},{8,9},{9,10},{10,1... | collective-permute-start | bytes 442376 | tf_op jit(solution)/shard_map/ppermute | solution.py:20
  69.2 12.7 %collective-permute-start.5 = (bf16[6,96,1,128]{1,2,3,0:T(2,128)(2,1)S(1)}, bf16[6,96,1,128]{1,2,3,0:T(2,128)(2,1)S(1)}, u32[]{:S(2)}, u32[]{:S(2)}) collective-permute-start(bf16[6,96,1,128]{1,2,3,0:T(2,128)(2,1)S(1)} %get-tuple-element.15), channel_id=1, source_target_pairs={{1,0},{2,1},{3,2},{4,3},{5,4},{6,5},{7,6},{8,7},{9,8},{10,9},{11,1... | collective-permute-start | bytes 442376 | tf_op jit(solution)/shard_map/ppermute | solution.py:21
  87.8 1.1 %copy-start.10 = (bf16[3,3,3,96,96]{4,3,2,1,0:T(8,128)(2,1)S(1)}, bf16[3,3,3,96,96]{4,3,2,1,0:T(8,128)(2,1)}, u32[]{:S(2)}) copy-start(bf16[3,3,3,96,96]{4,3,2,1,0:T(8,128)(2,1)} %param.18) | copy-start | bytes 1492996
  90.5 1.6 %copy-start.6 = (f32[4,4,136,96]{3,0,2,1:T(4,128)S(1)}, f32[4,4,136,96]{3,0,2,1:T(4,128)}, u32[]{:S(2)}) copy-start(f32[4,4,136,96]{3,0,2,1:T(4,128)} %copy-done.5) | copy-start | bytes 2506756
  90.5 1.6 %copy-start.12 = (f32[96]{0:T(128)S(1)}, f32[96]{0:T(128)}, u32[]{:S(2)}) copy-start(f32[96]{0:T(128)} %param.19) | copy-start | bytes 1156
  94.4 1.1 %copy-start.2 = (bf16[4,192,4,128]{3,2,1,0:T(4,128)(2,1)S(1)}, bf16[4,192,4,128]{3,2,1,0:T(4,128)(2,1)}, u32[]{:S(2)}) copy-start(bf16[4,192,4,128]{3,2,1,0:T(4,128)(2,1)} %param.12) | copy-start | bytes 2359300
  94.4 1.1 %copy-start.7 = (f32[96]{0:T(128)S(1)}, f32[96]{0:T(128)}, u32[]{:S(2)}) copy-start(f32[96]{0:T(128)} %param.21) | copy-start | bytes 1156
where the time goes:
time: 97.3 us; the launch traced here: 96.8 us
  waiting for transfers between devices  29.2 us (30%)
  local copies, waits for them, and re-layouts  22.4 us (23%)
  starting transfers between devices  16.9 us (17%)
  matrix products  13.9 us (14%)
  other arithmetic  13.8 us (14%)
    conv_general_dilated x6, matrix products, causal_conv(): lax.conv_general_dilated(slab, weight[t_tap], (1, 1), ((0, 0), (1, 1)), d...  13.6 us
    ppermute x2, waiting for transfers between devices, passed_along(): return lax.ppermute(block, axis, route)  10.9 us
    unnamed x35, local copies, waits for them, and re-layouts  9.8 us
    ppermute x2, waiting for transfers between devices, padded_2(): before = lax.ppermute(last, axis, up)  9.24 us
    ppermute x2, waiting for transfers between devices, padded_2(): after = lax.ppermute(first, axis, down)  9.06 us
    ppermute x2, starting transfers between devices, padded_2(): before = lax.ppermute(last, axis, up)  8.86 us
    conv_general_dilated x6, other arithmetic, causal_conv(): lax.conv_general_dilated(slab, weight[t_tap], (1, 1), ((0, 0), (1, 1)), d...  6.36 us
    slice x8, local copies, waits for them, and re-layouts, causal_conv(): slab = padded[t_tap:t_tap + out_frames]  6.17 us
  transfers between devices with their start and end apart: 6, of which 6 were waited for; matrix products, arithmetic and copies ran while one was open for 2% of the time, Pallas kernels for 0%

commit v1 on v0

v1 whole, which is shorter than its diff:
```python
import jax
import jax.numpy as jnp
from jax import lax
from jax.experimental import pallas as pl
from jax.experimental.pallas import tpu as pltpu
from jax.sharding import PartitionSpec as P

MESH = pl.DeviceIdType.MESH
F32 = jnp.float32
BF16 = jnp.bfloat16
EPS = 1e-6
LANES = 128
PARTS = ((1, 2), (0, 3))


def column(row_ref, scale=1.0):
    size = row_ref.shape[1]
    down = lax.broadcasted_iota(jnp.int32, (size, size), 0)
    across = lax.broadcasted_iota(jnp.int32, (size, size), 1)
    picked = jnp.where(down == across, row_ref[...] * scale, 0.0)
    return jnp.broadcast_to(jnp.sum(picked, axis=1, keepdims=True), (size, LANES))


def norm_silu(values, half_gain):
    mean_sq = jnp.mean(values * values, axis=0, keepdims=True)
    half = values * lax.rsqrt(mean_sq + EPS) * half_gain
    return half + half * jnp.tanh(half)


def put_shifts(x_ref, frame, row, values):
    lane = lax.broadcasted_iota(jnp.int32, values.shape, 1)
    left = jnp.where(lane == 0, 0.0, pltpu.roll(values, 1, 1))
    right = jnp.where(lane == LANES - 1, 0.0, pltpu.roll(values, LANES - 1, 1))
    x_ref[frame, row, 0] = left.astype(BF16)
    x_ref[frame, row, 2] = right.astype(BF16)


def body(
    n_t,
    n_r,
    latent_hbm,
    clips,
    gain_in,
    conv_in_hbm,
    bias_in,
    gain_mid,
    conv_mid_hbm,
    bias_mid,
    skip_hbm,
    skip_bias,
    out_hbm,
    latent_v,
    wide,
    raw,
    x1,
    x2,
    taps1,
    taps2,
    w1,
    w2,
    w_skip,
    col_in,
    col_bias,
    col_mid,
    col_out,
    acc1,
    acc2,
    sent1,
    got1,
    sent2,
    got2,
    packed,
    out_v,
    load_sem,
    store_sem,
    row_send,
    row_recv,
    time_send,
    time_recv,
):
    t_at = lax.axis_index("tm")
    r_at = lax.axis_index("rows")
    up, down = lax.rem(r_at + n_r - 1, n_r), lax.rem(r_at + 1, n_r)
    before, after = lax.rem(t_at + n_t - 1, n_t), lax.rem(t_at + 1, n_t)

    loads = {}
    for k, frame in enumerate((2, 3, 0, 1)):
        loads[frame] = pltpu.make_async_copy(latent_hbm.at[frame], latent_v.at[frame], load_sem.at[k])
    for k, (src, dst) in enumerate(((conv_in_hbm, taps1), (conv_mid_hbm, taps2), (skip_hbm, w_skip))):
        loads["w%d" % k] = pltpu.make_async_copy(src, dst, load_sem.at[4 + k])
    for copy in loads.values():
        copy.start()

    barrier = pltpu.get_barrier_semaphore()
    for peer in ({"rows": up}, {"rows": down}, {"tm": before}, {"tm": after}):
        pl.semaphore_signal(barrier, inc=1, device_id=peer, device_id_type=MESH)

    total = clips.shape[0]

    def keep(frame, back):
        at = t_at * 4 + frame
        own = clips[jnp.minimum(at, total - 1)]
        past = clips[jnp.clip(at - back, 0, total - 1)]
        good = (own == past) & (at < total) & (at >= back)
        return jnp.where(good, 1.0, 0.0).astype(F32)

    keeps = {(f, d): keep(f, d) for f in range(1, 6) for d in (1, 2) if 0 <= f - d < 4}
    live = {0: jnp.where(r_at > 0, 1.0, 0.0).astype(F32), 5: jnp.where(r_at < n_r - 1, 1.0, 0.0).astype(F32)}

    col_in[...] = column(gain_in, 0.5)
    col_bias[...] = column(bias_in)
    col_mid[...] = column(gain_mid, 0.5)
    col_out[...] = column(bias_mid) + column(skip_bias)

    def row_copies(x_ref, first, slot):
        pair = pl.ds(first, 2)
        return [
            pltpu.make_async_remote_copy(
                src_ref=x_ref.at[pair, mine, 1],
                dst_ref=x_ref.at[pair, theirs, 1],
                send_sem=row_send.at[slot + k],
                recv_sem=row_recv.at[slot + k],
                device_id={"rows": peer},
                device_id_type=MESH,
            )
            for k, (mine, theirs, peer) in enumerate(((1, 5, up), (4, 0, down)))
        ]

    def time_copy(src, dst, part, slot):
        return pltpu.make_async_remote_copy(
            src_ref=src.at[part],
            dst_ref=dst.at[part],
            send_sem=time_send.at[slot],
            recv_sem=time_recv.at[slot],
            device_id={"tm": after},
            device_id_type=MESH,
        )

    rows1 = {2: row_copies(x1, 2, 0), 0: row_copies(x1, 0, 2)}
    rows2 = {2: row_copies(x2, 2, 4), 0: row_copies(x2, 0, 6)}
    times1 = [time_copy(sent1, got1, part, part) for part in range(2)]
    times2 = [time_copy(sent2, got2, part, 2 + part) for part in range(2)]

    def start(copies):
        for copy in copies:
            copy.start()

    def first_act(frame, rows):
        for row in rows:
            values = wide[frame, pl.ds(row, 192, stride=4), :]
            raw[frame, row] = values.astype(BF16)
            act = norm_silu(values, col_in[...])
            x1[frame, row + 1, 1] = act.astype(BF16)
            put_shifts(x1, frame, row + 1, act)

    def halo(x_ref, copies, first):
        for row, copy in ((5, copies[0]), (0, copies[1])):
            copy.wait_recv()
            for frame in (first, first + 1):
                values = x_ref[frame, row, 1].astype(F32) * live[row]
                x_ref[frame, row, 1] = values.astype(BF16)
                put_shifts(x_ref, frame, row, values)

    seen = {}

    def conv(weight, x_ref, acc, first, rows, base):
        spots = [(f, r) for r in rows for f in (first, first + 1)]
        depth = 9 * x_ref.shape[3]
        slab = jnp.concatenate([x_ref[f, pl.ds(r, 3)].reshape(depth, LANES) for f, r in spots], axis=1)
        terms = jnp.dot(weight[...], slab, preferred_element_type=F32)
        sums = {}
        for k, (f, r) in enumerate(spots):
            for tap in range(3):
                value = terms[tap * 96 : (tap + 1) * 96, k * LANES : (k + 1) * LANES]
                target = f + 2 - tap
                if target > f:
                    value = value * keeps[target, target - f]
                key = (target, r)
                sums[key] = value if key not in sums else sums[key] + value
        for (target, r), value in sums.items():
            key = (id(acc), target, r)
            if key in seen:
                value = value + acc[target, r]
            elif target < 4 and base is not None:
                value = value + base
            seen[key] = True
            acc[target, r] = value

    def pass_on(acc, buf, copies, part):
        for g in range(2):
            for k, row in enumerate(PARTS[part]):
                buf[part, g, k] = acc[4 + g, row].astype(BF16)
        copies[part].start()

    def second_act(frame, part):
        for k, row in enumerate(PARTS[part]):
            values = acc1[frame, row]
            if frame < 2:
                values = values + got1[part, frame, k].astype(F32)
            act = norm_silu(values, col_mid[...])
            x2[frame, row + 1, 1] = act.astype(BF16)
            put_shifts(x2, frame, row + 1, act)

    def shortcut(rows):
        spots = [(f, r) for r in rows for f in range(4)]
        slab = jnp.concatenate([raw[f, r] for f, r in spots], axis=1)
        terms = jnp.dot(w_skip[...], slab, preferred_element_type=F32)
        for k, (f, r) in enumerate(spots):
            acc2[f, r] = terms[:, k * LANES : (k + 1) * LANES] + col_out[...]
            seen[id(acc2), f, r] = True

    def finish(frame):
        for part in range(2):
            for k, row in enumerate(PARTS[part]):
                values = acc2[frame, row]
                if frame < 2:
                    values = values + got2[part, frame, k].astype(F32)
                packed[frame, pl.ds(row, 96, stride=4), :] = values
        out_v[frame] = packed[frame].astype(BF16)
        copy = pltpu.make_async_copy(out_v.at[frame], out_hbm.at[frame], store_sem.at[frame])
        copy.start()
        return copy

    for frame in (2, 3):
        loads[frame].wait()
        wide[frame] = latent_v[frame].astype(F32)
        first_act(frame, (0, 3))
    pl.semaphore_wait(barrier, 4)
    start(rows1[2])
    for frame in (0, 1):
        loads[frame].wait()
        wide[frame] = latent_v[frame].astype(F32)
        first_act(frame, (0, 3))
    start(rows1[0])
    for k in range(3):
        loads["w%d" % k].wait()
    for tap in range(3):
        w1[pl.ds(tap * 96, 96), :] = jnp.concatenate([taps1[tap * 9 + k] for k in range(9)], axis=1)
        w2[pl.ds(tap * 96, 96), :] = jnp.concatenate([taps2[tap * 9 + k] for k in range(9)], axis=1)
    for frame in (2, 3, 0, 1):
        first_act(frame, (1, 2))

    conv(w1, x1, acc1, 2, (1, 2), col_bias[...])
    pass_on(acc1, sent1, times1, 0)
    conv(w1, x1, acc1, 0, (1, 2), col_bias[...])
    for row in range(4):
        shortcut((row,))
    halo(x1, rows1[2], 2)
    conv(w1, x1, acc1, 2, (0, 3), col_bias[...])
    pass_on(acc1, sent1, times1, 1)
    halo(x1, rows1[0], 0)
    conv(w1, x1, acc1, 0, (0, 3), col_bias[...])

    for frame in (2, 3):
        second_act(frame, 1)
    start(rows2[2])
    for frame in (2, 3):
        second_act(frame, 0)
    conv(w2, x2, acc2, 2, (1, 2), None)
    pass_on(acc2, sent2, times2, 0)
    times1[1].wait_recv()
    for frame in (0, 1):
        second_act(frame, 1)
    start(rows2[0])
    times1[0].wait_recv()
    for frame in (0, 1):
        second_act(frame, 0)
    conv(w2, x2, acc2, 0, (1, 2), None)
    halo(x2, rows2[2], 2)
    conv(w2, x2, acc2, 2, (0, 3), None)
    pass_on(acc2, sent2, times2, 1)
    halo(x2, rows2[0], 0)
    conv(w2, x2, acc2, 0, (0, 3), None)
    stores = [finish(2), finish(3)]
    times2[0].wait_recv()
    times2[1].wait_recv()
    stores += [finish(0), finish(1)]
    for copy in stores:
        copy.wait()
    for copy in rows1[2] + rows1[0] + rows2[2] + rows2[0] + times1 + times2:
        copy.wait_send()


def block(n_t, n_r, latent, clips, gain_in, conv_in, bias_in, gain_mid, conv_mid, bias_mid, skip_weight, skip_bias):
    hbm = pl.BlockSpec(memory_space=pl.ANY)
    vmem = pl.BlockSpec(memory_space=pltpu.VMEM)
    smem = pl.BlockSpec(memory_space=pltpu.SMEM)
    dma = pltpu.SemaphoreType.DMA
    out = pl.pallas_call(
        lambda *refs: body(n_t, n_r, *refs),
        out_shape=jax.ShapeDtypeStruct((4, 384, LANES), BF16),
        in_specs=[hbm, smem, vmem, hbm, vmem, vmem, hbm, vmem, hbm, vmem],
        out_specs=hbm,
        scratch_shapes=[
            pltpu.VMEM((4, 768, LANES), BF16),
            pltpu.VMEM((4, 768, LANES), F32),
            pltpu.VMEM((4, 4, 192, LANES), BF16),
            pltpu.VMEM((4, 6, 3, 192, LANES), BF16),
            pltpu.VMEM((4, 6, 3, 96, LANES), BF16),
            pltpu.VMEM((27, 96, 192), BF16),
            pltpu.VMEM((27, 96, 96), BF16),
            pltpu.VMEM((288, 1728), BF16),
            pltpu.VMEM((288, 864), BF16),
            pltpu.VMEM((96, 192), BF16),
            pltpu.VMEM((192, LANES), F32),
            pltpu.VMEM((96, LANES), F32),
            pltpu.VMEM((96, LANES), F32),
            pltpu.VMEM((96, LANES), F32),
            pltpu.VMEM((6, 4, 96, LANES), F32),
            pltpu.VMEM((6, 4, 96, LANES), F32),
            pltpu.VMEM((2, 2, 2, 96, LANES), BF16),
            pltpu.VMEM((2, 2, 2, 96, LANES), BF16),
            pltpu.VMEM((2, 2, 2, 96, LANES), BF16),
            pltpu.VMEM((2, 2, 2, 96, LANES), BF16),
            pltpu.VMEM((4, 384, LANES), F32),
            pltpu.VMEM((4, 384, LANES), BF16),
            dma((7,)),
            dma((4,)),
            dma((8,)),
            dma((8,)),
            dma((4,)),
            dma((4,)),
        ],
        compiler_params=pltpu.CompilerParams(
            collective_id=0, has_side_effects=True, vmem_limit_bytes=40 * 1024 * 1024
        ),
        name="residual_block",
    )(
        latent.reshape(4, 768, LANES),
        clips,
        gain_in.reshape(1, 192),
        conv_in.reshape(27, 96, 192),
        bias_in.reshape(1, 96),
        gain_mid.reshape(1, 96),
        conv_mid.reshape(27, 96, 96),
        bias_mid.reshape(1, 96),
        skip_weight,
        skip_bias.reshape(1, 96),
    )
    return out.reshape(4, 96, 4, LANES)


def solution(mesh):
    n_t, n_r = mesh.shape["tm"], mesh.shape["rows"]
    return jax.shard_map(
        lambda *args: block(n_t, n_r, *args),
        mesh=mesh,
        in_specs=(P("tm", None, "rows", None),) + (P(),) * 9,
        out_specs=P("tm", None, "rows", None),
        check_vma=False,
    )
```

time: 97.3 us -> 36.3 us (0.37)
  the two profiles are of different devices: /device:TPU:50 before, /device:TPU:1 now
where the time goes in v1:
time: 36.3 us; the launch traced here: 36 us
  Pallas kernels  27 us (74%)
  local copies, waits for them, and re-layouts  9.04 us (25%)
    pallas_call x1, Pallas kernels, block(): pl.pallas_call(lambda *refs: body(n_t, n_r, *refs), out_shape=jax.ShapeDt...  27 us
    unnamed x21, local copies, waits for them, and re-layouts  9.04 us

profile of v1, /device:TPU:1, one launch (start us, length us, event | category | flops | bytes accessed | tf_op | source)
XLA Modules:
  0.0 36.0 jit_solution(1313967202658703319)
XLA Ops:
  0.0 0.0 copy-start
  0.0 1.3 %copy-done = bf16[3,3,3,96,192]{4,3,2,1,0:T(8,128)(2,1)S(1)} copy-done((bf16[3,3,3,96,192]{4,3,2,1,0:T(8,128)(2,1)S(1)}, bf16[3,3,3,96,192]{4,3,2,1,0:T(8,128)(2,1)}, u32[]{:S(2)}) %copy-start) | copy-done | bytes 995352
  1.3 0.0 copy-start.1
  1.3 1.1 %copy-done.1 = bf16[4,192,4,128]{3,2,1,0:T(4,128)(2,1)S(1)} copy-done((bf16[4,192,4,128]{3,2,1,0:T(4,128)(2,1)S(1)}, bf16[4,192,4,128]{3,2,1,0:T(4,128)(2,1)}, u32[]{:S(2)}) %copy-start.1) | copy-done | bytes 786456
  2.5 0.0 copy-start.2
  2.5 1.1 %copy-done.2 = bf16[3,3,3,96,96]{4,3,2,1,0:T(8,128)(2,1)S(1)} copy-done((bf16[3,3,3,96,96]{4,3,2,1,0:T(8,128)(2,1)S(1)}, bf16[3,3,3,96,96]{4,3,2,1,0:T(8,128)(2,1)}, u32[]{:S(2)}) %copy-start.2) | copy-done | bytes 497688
  3.5 0.0 copy-start.3
  3.5 0.8 %copy-done.3 = bf16[96,192]{1,0:T(8,128)(2,1)S(1)} copy-done((bf16[96,192]{1,0:T(8,128)(2,1)S(1)}, bf16[96,192]{1,0:T(8,128)(2,1)}, u32[]{:S(2)}) %copy-start.3) | copy-done | bytes 36888
  4.3 0.0 copy-start.4
  4.3 0.7 %copy-done.4 = f32[192]{0:T(256)S(1)} copy-done((f32[192]{0:T(256)S(1)}, f32[192]{0:T(256)}, u32[]{:S(2)}) %copy-start.4) | copy-done | bytes 792
  5.0 0.0 copy-start.5
  5.0 0.7 %copy-done.5 = s32[32]{0:T(128)S(1)} copy-done((s32[32]{0:T(128)S(1)}, s32[32]{0:T(128)}, u32[]{:S(2)}) %copy-start.5) | copy-done | bytes 152
  5.7 0.0 copy-start.6
  5.7 0.7 %copy-done.6 = f32[96]{0:T(128)S(1)} copy-done((f32[96]{0:T(128)S(1)}, f32[96]{0:T(128)}, u32[]{:S(2)}) %copy-start.6) | copy-done | bytes 408
  6.3 0.0 copy-start.7
  6.3 0.7 %copy-done.7 = f32[96]{0:T(128)S(1)} copy-done((f32[96]{0:T(128)S(1)}, f32[96]{0:T(128)}, u32[]{:S(2)}) %copy-start.7) | copy-done | bytes 408
  7.0 0.0 copy-start.8
  7.0 0.7 %copy-done.8 = f32[96]{0:T(128)S(1)} copy-done((f32[96]{0:T(128)S(1)}, f32[96]{0:T(128)}, u32[]{:S(2)}) %copy-start.8) | copy-done | bytes 408
  7.6 0.0 copy-start.9
  7.7 0.7 %copy-done.9 = f32[96]{0:T(128)S(1)} copy-done((f32[96]{0:T(128)S(1)}, f32[96]{0:T(128)}, u32[]{:S(2)}) %copy-start.9) | copy-done | bytes 408
  8.3 27.0 %residual_block.1 = bf16[4,384,128]{2,1,0:T(8,128)(2,1)S(1)} custom-call(bf16[4,768,128]{2,1,0:T(8,128)(2,1)S(1)} %bitcast.11, s32[32]{0:T(128)S(1)} %copy-done.5, f32[1,192]{1,0:T(1,128)S(1)} %bitcast.13, bf16[27,96,192]{2,1,0:T(8,128)(2,1)S(1)} %bitcast.10, f32[1,96]{1,0:T(1,128)S(1)} %bitcast.14, f32[1,96]{1,0:T(1,128)S(1)} %bitcast.15, ...), custom_call_target="tpu_custom_call" | custom-call | tf_op jit(solution)/shard_map/residual_block/pallas_call | solution.py:289
  35.3 0.7 %copy.12 = bf16[4,96,4,128]{3,2,1,0:T(4,128)(2,1)} copy(bf16[4,96,4,128]{3,2,1,0:T(4,128)(2,1)S(1)} %bitcast.9) | data formatting | bytes 786432
Async XLA Ops:
  0.0 1.3 %copy-start = (bf16[3,3,3,96,192]{4,3,2,1,0:T(8,128)(2,1)S(1)}, bf16[3,3,3,96,192]{4,3,2,1,0:T(8,128)(2,1)}, u32[]{:S(2)}) copy-start(bf16[3,3,3,96,192]{4,3,2,1,0:T(8,128)(2,1)} %param.13) | copy-start | bytes 2985988
  1.3 1.1 %copy-start.1 = (bf16[4,192,4,128]{3,2,1,0:T(4,128)(2,1)S(1)}, bf16[4,192,4,128]{3,2,1,0:T(4,128)(2,1)}, u32[]{:S(2)}) copy-start(bf16[4,192,4,128]{3,2,1,0:T(4,128)(2,1)} %param.10) | copy-start | bytes 2359300
  2.5 1.1 %copy-start.2 = (bf16[3,3,3,96,96]{4,3,2,1,0:T(8,128)(2,1)S(1)}, bf16[3,3,3,96,96]{4,3,2,1,0:T(8,128)(2,1)}, u32[]{:S(2)}) copy-start(bf16[3,3,3,96,96]{4,3,2,1,0:T(8,128)(2,1)} %param.16) | copy-start | bytes 1492996
  3.5 0.8 %copy-start.3 = (bf16[96,192]{1,0:T(8,128)(2,1)S(1)}, bf16[96,192]{1,0:T(8,128)(2,1)}, u32[]{:S(2)}) copy-start(bf16[96,192]{1,0:T(8,128)(2,1)} %refs_8_.1) | copy-start | bytes 110596
  4.3 0.7 %copy-start.4 = (f32[192]{0:T(256)S(1)}, f32[192]{0:T(256)}, u32[]{:S(2)}) copy-start(f32[192]{0:T(256)} %param.12) | copy-start | bytes 2308
  5.0 0.7 %copy-start.5 = (s32[32]{0:T(128)S(1)}, s32[32]{0:T(128)}, u32[]{:S(2)}) copy-start(s32[32]{0:T(128)} %refs_1_.1) | copy-start | bytes 388
  5.7 0.7 %copy-start.6 = (f32[96]{0:T(128)S(1)}, f32[96]{0:T(128)}, u32[]{:S(2)}) copy-start(f32[96]{0:T(128)} %param.14) | copy-start | bytes 1156
  6.3 0.7 %copy-start.7 = (f32[96]{0:T(128)S(1)}, f32[96]{0:T(128)}, u32[]{:S(2)}) copy-start(f32[96]{0:T(128)} %param.15) | copy-start | bytes 1156
  7.0 0.7 %copy-start.8 = (f32[96]{0:T(128)S(1)}, f32[96]{0:T(128)}, u32[]{:S(2)}) copy-start(f32[96]{0:T(128)} %param.17) | copy-start | bytes 1156
  7.6 0.7 %copy-start.9 = (f32[96]{0:T(128)S(1)}, f32[96]{0:T(128)}, u32[]{:S(2)}) copy-start(f32[96]{0:T(128)} %param.19) | copy-start | bytes 1156

commit v2 on v1

--- a/solution.py
+++ b/solution.py
@@ -39,16 +39,22 @@
     n_t,
     n_r,
     latent_hbm,
+    clips_hbm,
+    gain_in_hbm,
+    conv_in_hbm,
+    bias_in_hbm,
+    gain_mid_hbm,
+    conv_mid_hbm,
+    bias_mid_hbm,
+    skip_hbm,
+    skip_bias_hbm,
+    out_hbm,
     clips,
     gain_in,
-    conv_in_hbm,
     bias_in,
     gain_mid,
-    conv_mid_hbm,
     bias_mid,
-    skip_hbm,
     skip_bias,
-    out_hbm,
     latent_v,
     wide,
     raw,
@@ -88,13 +94,24 @@
         loads[frame] = pltpu.make_async_copy(latent_hbm.at[frame], latent_v.at[frame], load_sem.at[k])
     for k, (src, dst) in enumerate(((conv_in_hbm, taps1), (conv_mid_hbm, taps2), (skip_hbm, w_skip))):
         loads["w%d" % k] = pltpu.make_async_copy(src, dst, load_sem.at[4 + k])
-    for copy in loads.values():
+    small = (
+        (clips_hbm, clips),
+        (gain_in_hbm, gain_in),
+        (bias_in_hbm, bias_in),
+        (gain_mid_hbm, gain_mid),
+        (bias_mid_hbm, bias_mid),
+        (skip_bias_hbm, skip_bias),
+    )
+    small = [pltpu.make_async_copy(src, dst, load_sem.at[7 + k]) for k, (src, dst) in enumerate(small)]
+    for copy in small + list(loads.values()):
         copy.start()
 
     barrier = pltpu.get_barrier_semaphore()
     for peer in ({"rows": up}, {"rows": down}, {"tm": before}, {"tm": after}):
         pl.semaphore_signal(barrier, inc=1, device_id=peer, device_id_type=MESH)
 
+    for copy in small:
+        copy.wait()
     total = clips.shape[0]
 
     def keep(frame, back):
@@ -282,16 +299,20 @@
 
 
 def block(n_t, n_r, latent, clips, gain_in, conv_in, bias_in, gain_mid, conv_mid, bias_mid, skip_weight, skip_bias):
-    hbm = pl.BlockSpec(memory_space=pl.ANY)
-    vmem = pl.BlockSpec(memory_space=pltpu.VMEM)
-    smem = pl.BlockSpec(memory_space=pltpu.SMEM)
+    hbm = pl.BlockSpec(memory_space=pltpu.HBM)
     dma = pltpu.SemaphoreType.DMA
     out = pl.pallas_call(
         lambda *refs: body(n_t, n_r, *refs),
         out_shape=jax.ShapeDtypeStruct((4, 384, LANES), BF16),
-        in_specs=[hbm, smem, vmem, hbm, vmem, vmem, hbm, vmem, hbm, vmem],
-        out_specs=hbm,
+        in_specs=[hbm] * 10,
+        out_specs=pl.BlockSpec(memory_space=pl.ANY),
         scratch_shapes=[
+            pltpu.SMEM(clips.shape, jnp.int32),
+            pltpu.VMEM((1, 192), F32),
+            pltpu.VMEM((1, 96), F32),
+            pltpu.VMEM((1, 96), F32),
+            pltpu.VMEM((1, 96), F32),
+            pltpu.VMEM((1, 96), F32),
             pltpu.VMEM((4, 768, LANES), BF16),
             pltpu.VMEM((4, 768, LANES), F32),
             pltpu.VMEM((4, 4, 192, LANES), BF16),
@@ -314,7 +335,7 @@
             pltpu.VMEM((2, 2, 2, 96, LANES), BF16),
             pltpu.VMEM((4, 384, LANES), F32),
             pltpu.VMEM((4, 384, LANES), BF16),
-            dma((7,)),
+            dma((13,)),
             dma((4,)),
             dma((8,)),
             dma((8,)),
@@ -322,7 +343,7 @@
             dma((4,)),
         ],
         compiler_params=pltpu.CompilerParams(
-            collective_id=0, has_side_effects=True, vmem_limit_bytes=40 * 1024 * 1024
+            collective_id=0, has_side_effects=True, vmem_limit_bytes=64 * 1024 * 1024
         ),
         name="residual_block",
     )(

time: 36.3 us -> 27.4 us (0.75)
  local copies, waits for them, and re-layouts: 9.04 us -> 1.88 us
  Pallas kernels: 27 us -> 25.4 us
    unnamed x21 -> x1, local copies, waits for them, and re-layouts: 9.04 us -> 1.88 us
    pallas_call x1, Pallas kernels: 27 us -> 25.4 us  [block(): pl.pallas_call(lambda *refs: body(n_t, n_r, *refs), out_shape=jax.ShapeDt...]
where the time goes in v2:
time: 27.4 us; the launch traced here: 27.3 us
  Pallas kernels  25.4 us (93%)
  local copies, waits for them, and re-layouts  1.88 us (7%)
    pallas_call x1, Pallas kernels, block(): pl.pallas_call(lambda *refs: body(n_t, n_r, *refs), out_shape=jax.ShapeDt...  25.4 us
    unnamed x1, local copies, waits for them, and re-layouts  1.88 us

profile of v2, /device:TPU:1, one launch (start us, length us, event | category | flops | bytes accessed | tf_op | source)
XLA Modules:
  0.0 27.3 jit_solution(6253179671557361003)
XLA Ops:
  0.0 25.4 %residual_block.1 = bf16[4,384,128]{2,1,0:T(8,128)(2,1)} custom-call(bf16[4,768,128]{2,1,0:T(8,128)(2,1)} %bitcast.11, s32[32]{0:T(128)} %refs_1_.1, f32[1,192]{1,0:T(1,128)} %bitcast.13, bf16[27,96,192]{2,1,0:T(8,128)(2,1)} %bitcast.10, f32[1,96]{1,0:T(1,128)} %bitcast.14, f32[1,96]{1,0:T(1,128)} %bitcast.15, bf16[27,96,96]{2,1,0:T(8,128)(2,1)} %bitcast.12, ...), custom_call_target="tpu_custom_call" | custom-call | tf_op jit(solution)/shard_map/residual_block/pallas_call | solution.py:304
  25.4 1.9 %copy.12 = bf16[4,96,4,128]{3,2,1,0:T(4,128)(2,1)} copy(bf16[4,96,4,128]{3,2,1,0:T(4,128)(2,1)} %bitcast.9) | data formatting | bytes 786432

commit v3 on v2

v3 whole, which is shorter than its diff:
```python
import jax
import jax.numpy as jnp
from jax import lax
from jax.experimental import pallas as pl
from jax.experimental.pallas import tpu as pltpu
from jax.sharding import PartitionSpec as P

MESH = pl.DeviceIdType.MESH
F32 = jnp.float32
BF16 = jnp.bfloat16
EPS = 1e-6
LANES = 128
PARTS = ((1, 2), (0, 3))


def column(row_ref, scale=1.0):
    size = row_ref.shape[1]
    down = lax.broadcasted_iota(jnp.int32, (size, size), 0)
    across = lax.broadcasted_iota(jnp.int32, (size, size), 1)
    picked = jnp.where(down == across, row_ref[...] * scale, 0.0)
    return jnp.broadcast_to(jnp.sum(picked, axis=1, keepdims=True), (size, LANES))


def norm_silu(values, half_gain):
    mean_sq = jnp.mean(values * values, axis=0, keepdims=True)
    half = values * lax.rsqrt(mean_sq + EPS) * half_gain
    return half + half * jnp.tanh(half)


def put_shifts(x_ref, frame, row, values):
    lane = lax.broadcasted_iota(jnp.int32, values.shape, 1)
    left = jnp.where(lane == 0, 0.0, pltpu.roll(values, 1, 1))
    right = jnp.where(lane == LANES - 1, 0.0, pltpu.roll(values, LANES - 1, 1))
    x_ref[frame, row, 0] = left.astype(BF16)
    x_ref[frame, row, 2] = right.astype(BF16)


class Exchange:
    def __init__(self, copies, sends, receives):
        self.copies, self.sends, self.receives = copies, sends, receives

    def start(self):
        @pl.when(self.sends)
        def _():
            for copy in self.copies:
                copy.start()

    def wait_recv(self):
        @pl.when(self.receives)
        def _():
            for copy in self.copies:
                copy.wait_recv()

    def wait_send(self):
        @pl.when(self.sends)
        def _():
            for copy in self.copies:
                copy.wait_send()


def body(
    n_t,
    n_r,
    latent_hbm,
    clips_hbm,
    gain_in_hbm,
    conv_in_hbm,
    bias_in_hbm,
    gain_mid_hbm,
    conv_mid_hbm,
    bias_mid_hbm,
    skip_hbm,
    skip_bias_hbm,
    out_ref,
    clips,
    gain_in,
    bias_in,
    gain_mid,
    bias_mid,
    skip_bias,
    latent_v,
    wide,
    raw,
    x1,
    x2,
    taps1,
    taps2,
    w1,
    w1_low,
    w2,
    w_skip,
    col_in,
    col_bias,
    col_mid,
    col_out,
    acc1,
    acc2,
    edge_out,
    edge_in,
    sent1,
    got1,
    sent2,
    got2,
    packed,
    load_sem,
    row_send,
    row_recv,
    time_send,
    time_recv,
):
    t_at = lax.axis_index("tm")
    r_at = lax.axis_index("rows")
    has_up, has_down = r_at > 0, r_at < n_r - 1
    has_before, has_after = t_at > 0, t_at < n_t - 1
    up, down, before, after = {"rows": r_at - 1}, {"rows": r_at + 1}, {"tm": t_at - 1}, {"tm": t_at + 1}

    barrier = pltpu.get_barrier_semaphore()
    for there, peer in ((has_up, up), (has_down, down), (has_before, before)):

        @pl.when(there)
        def _(peer=peer):
            pl.semaphore_signal(barrier, inc=1, device_id=peer, device_id_type=MESH)

    pairs = [(latent_hbm.at[f], latent_v.at[f]) for f in (2, 3, 0, 1)]
    pairs += [(conv_in_hbm, taps1), (gain_in_hbm, gain_in), (clips_hbm, clips), (bias_in_hbm, bias_in)]
    pairs += [(gain_mid_hbm, gain_mid), (bias_mid_hbm, bias_mid), (skip_bias_hbm, skip_bias)]
    pairs += [(skip_hbm, w_skip), (conv_mid_hbm, taps2)]
    order = [0, 1, 5, 4, 2, 3, 6, 7, 8, 9, 10, 11, 12]
    loads = [pltpu.make_async_copy(src, dst, load_sem.at[k]) for k, (src, dst) in enumerate(pairs)]
    for k in order:
        loads[k].start()
    latent_load = {2: loads[0], 3: loads[1], 0: loads[2], 1: loads[3]}

    @pl.when(jnp.logical_not(has_up))
    def _():
        edge_in[1] = jnp.zeros(edge_in.shape[1:], BF16)
        x2[:, 0] = jnp.zeros((4, 3, 96, LANES), BF16)

    @pl.when(jnp.logical_not(has_down))
    def _():
        edge_in[0] = jnp.zeros(edge_in.shape[1:], BF16)
        x2[:, 5] = jnp.zeros((4, 3, 96, LANES), BF16)

    @pl.when(jnp.logical_not(has_before))
    def _():
        got1[...] = jnp.zeros(got1.shape, BF16)
        got2[...] = jnp.zeros(got2.shape, BF16)

    def remote(src, dst, send_sem, recv_sem, peer):
        return pltpu.make_async_remote_copy(
            src_ref=src, dst_ref=dst, send_sem=send_sem, recv_sem=recv_sem, device_id=peer, device_id_type=MESH
        )

    def by_row(src_of, dst_of, slot):
        return [
            Exchange([remote(src_of(k), dst_of(k), row_send.at[slot + k], row_recv.at[slot + k], peer)], sends, gets)
            for k, (peer, sends, gets) in enumerate(((up, has_up, has_down), (down, has_down, has_up)))
        ]

    def by_time(src, dst, part, slot):
        copy = remote(src.at[part], dst.at[part], time_send.at[slot], time_recv.at[slot], after)
        return Exchange([copy], has_after, has_before)

    rows1 = {g: by_row(lambda k: edge_out.at[k, pl.ds(g, 2)], lambda k: edge_in.at[k, pl.ds(g, 2)], g) for g in (4, 2, 0)}
    rows2 = {
        f: by_row(lambda k: x2.at[pl.ds(f, 2), (1, 4)[k], 1], lambda k: x2.at[pl.ds(f, 2), (5, 0)[k], 1], 6 + f)
        for f in (2, 0)
    }
    times1 = [by_time(sent1, got1, part, part) for part in range(2)]
    times2 = [by_time(sent2, got2, part, 2 + part) for part in range(2)]

    def start(copies):
        for copy in copies:
            copy.start()

    def arrived(copies):
        for copy in copies:
            copy.wait_recv()

    def spread(frame):
        latent_load[frame].wait()
        wide[frame] = latent_v[frame].astype(F32)

    def first_act(frame, rows):
        for row in rows:
            values = wide[frame, pl.ds(row, 192, stride=4), :]
            raw[frame, row] = values.astype(BF16)
            act = norm_silu(values, col_in[...])
            x1[frame, row, 1] = act.astype(BF16)
            put_shifts(x1, frame, row, act)

    seen = set()

    def gather(acc, spots, terms, base):
        sums = {}
        for k, (f, r) in enumerate(spots):
            for tap in range(3):
                value = terms[tap * 96 : (tap + 1) * 96, k * LANES : (k + 1) * LANES]
                target = f + 2 - tap
                if target > f:
                    value = value * keeps[target, target - f]
                key = (target, r)
                sums[key] = value if key not in sums else sums[key] + value
        for (target, r), value in sums.items():
            key = (id(acc), target, r)
            if key in seen:
                value = value + acc[target, r]
            elif target < 4 and base is not None and 1 <= r <= 4:
                value = value + base
            seen.add(key)
            acc[target, r] = value

    def conv1(first, targets):
        taps = {-1: (0,), 0: (1, 0), 1: (0, 1, 2), 2: (1, 2, 3), 3: (2, 3), 4: (3,)}
        for target in targets:
            rows = taps[target]
            frames = (first, first + 1)
            slab = jnp.concatenate(
                [
                    jnp.concatenate([x1[f, row].reshape(576, LANES) for row in rows], axis=0)
                    for f in frames
                ],
                axis=1,
            )
            weight = w1_low if target < 1 else w1
            terms = jnp.dot(weight[:, : 576 * len(rows)], slab, preferred_element_type=F32)
            gather(acc1, [(f, target + 1) for f in frames], terms, col_bias[...])

    def conv2(first, rows):
        spots = [(f, r) for r in rows for f in (first, first + 1)]
        slab = jnp.concatenate([x2[f, pl.ds(r, 3)].reshape(864, LANES) for f, r in spots], axis=1)
        gather(acc2, spots, jnp.dot(w2[...], slab, preferred_element_type=F32), None)

    def edges_out(g):
        for k, row in enumerate((0, 5)):
            for frame in (g, g + 1):
                edge_out[k, frame] = acc1[frame, row].astype(BF16)
        start(rows1[g])

    def pass_on(value, buf, copies, part):
        for g in range(2):
            for k, row in enumerate(PARTS[part]):
                buf[part, g, k] = value(4 + g, row).astype(BF16)
        copies[part].start()

    def hidden(frame, row):
        values = acc1[frame, row + 1]
        if row in (0, 3):
            values = values + edge_in[1 if row == 0 else 0, frame].astype(F32)
        return values

    def second_act(frame, part):
        for k, row in enumerate(PARTS[part]):
            values = hidden(frame, row)
            if frame < 2:
                values = values + got1[part, frame, k].astype(F32)
            act = norm_silu(values, col_mid[...])
            x2[frame, row + 1, 1] = act.astype(BF16)
            put_shifts(x2, frame, row + 1, act)

    def halo2(first):
        arrived(rows2[first])
        for row in (0, 5):
            for frame in (first, first + 1):
                put_shifts(x2, frame, row, x2[frame, row, 1].astype(F32))

    def shortcut(row):
        slab = jnp.concatenate([raw[f, row] for f in range(4)], axis=1)
        terms = jnp.dot(w_skip[...], slab, preferred_element_type=F32)
        for f in range(4):
            acc2[f, row] = terms[:, f * LANES : (f + 1) * LANES] + col_out[...]
            seen.add((id(acc2), f, row))

    def finish(frame):
        for part in range(2):
            for k, row in enumerate(PARTS[part]):
                values = acc2[frame, row]
                if frame < 2:
                    values = values + got2[part, frame, k].astype(F32)
                packed[frame, pl.ds(row, 96, stride=4), :] = values
        out_ref[frame] = packed[frame].astype(BF16)

    loads[5].wait()
    col_in[...] = column(gain_in, 0.5)
    for frame in (2, 3):
        spread(frame)
        first_act(frame, (0, 3))
    loads[4].wait()
    for tap in range(3):
        at = pl.ds(tap * 96, 96)
        w1[at, :] = jnp.concatenate([taps1[tap * 9 + k] for k in range(9)], axis=1)
        w1_low[at, :] = jnp.concatenate([taps1[tap * 9 + k] for k in (6, 7, 8, 3, 4, 5)], axis=1)
    for k in (6, 7, 8, 9, 10):
        loads[k].wait()
    total = clips.shape[0]

    def keep(frame, back):
        at = t_at * 4 + frame
        own = clips[jnp.minimum(at, total - 1)]
        past = clips[jnp.clip(at - back, 0, total - 1)]
        good = (own == past) & (at < total) & (at >= back)
        return jnp.where(good, 1.0, 0.0).astype(F32)

    keeps = {(f, d): keep(f, d) for f in range(1, 6) for d in (1, 2) if 0 <= f - d < 4}
    col_bias[...] = column(bias_in)
    col_mid[...] = column(gain_mid, 0.5)
    col_out[...] = column(bias_mid) + column(skip_bias)

    conv1(2, (-1, 4))
    friends = has_up.astype(jnp.int32) + has_down.astype(jnp.int32) + has_after.astype(jnp.int32)
    pl.semaphore_wait(barrier, friends)
    edges_out(4)
    for frame in (0, 1):
        spread(frame)
        first_act(frame, (0, 3))
    conv1(0, (-1, 4))
    edges_out(2)
    edges_out(0)
    for frame in (2, 3):
        first_act(frame, (1, 2))
    conv1(2, (1, 2))
    pass_on(lambda g, row: acc1[g, row + 1], sent1, times1, 0)
    conv1(2, (0, 3))
    arrived(rows1[4])
    pass_on(hidden, sent1, times1, 1)
    for frame in (0, 1):
        first_act(frame, (1, 2))
    conv1(0, (0, 3, 1, 2))
    loads[12].wait()
    for tap in range(3):
        w2[pl.ds(tap * 96, 96), :] = jnp.concatenate([taps2[tap * 9 + k] for k in range(9)], axis=1)
    arrived(rows1[2])
    for frame in (2, 3):
        second_act(frame, 1)
    start(rows2[2])
    for frame in (2, 3):
        second_act(frame, 0)
    loads[11].wait()
    for row in range(4):
        shortcut(row)
    conv2(2, (1, 2))
    pass_on(lambda g, row: acc2[g, row], sent2, times2, 0)
    arrived(rows1[0])
    arrived(times1)
    for frame in (0, 1):
        second_act(frame, 1)
    start(rows2[0])
    for frame in (0, 1):
        second_act(frame, 0)
    conv2(0, (1, 2))
    halo2(2)
    conv2(2, (0, 3))
    pass_on(lambda g, row: acc2[g, row], sent2, times2, 1)
    halo2(0)
    conv2(0, (0, 3))
    finish(2)
    finish(3)
    arrived(times2)
    finish(0)
    finish(1)
    for copy in rows1[4] + rows1[2] + rows1[0] + rows2[2] + rows2[0] + times1 + times2:
        copy.wait_send()


def block(n_t, n_r, latent, clips, gain_in, conv_in, bias_in, gain_mid, conv_mid, bias_mid, skip_weight, skip_bias):
    hbm = pl.BlockSpec(memory_space=pltpu.HBM)
    dma = pltpu.SemaphoreType.DMA
    out = pl.pallas_call(
        lambda *refs: body(n_t, n_r, *refs),
        out_shape=pltpu.VMEM((4, 384, LANES), BF16),
        in_specs=[hbm] * 10,
        out_specs=pl.BlockSpec(memory_space=pltpu.VMEM),
        scratch_shapes=[
            pltpu.SMEM(clips.shape, jnp.int32),
            pltpu.VMEM((1, 192), F32),
            pltpu.VMEM((1, 96), F32),
            pltpu.VMEM((1, 96), F32),
            pltpu.VMEM((1, 96), F32),
            pltpu.VMEM((1, 96), F32),
            pltpu.VMEM((4, 768, LANES), BF16),
            pltpu.VMEM((4, 768, LANES), F32),
            pltpu.VMEM((4, 4, 192, LANES), BF16),
            pltpu.VMEM((4, 4, 3, 192, LANES), BF16),
            pltpu.VMEM((4, 6, 3, 96, LANES), BF16),
            pltpu.VMEM((27, 96, 192), BF16),
            pltpu.VMEM((27, 96, 96), BF16),
            pltpu.VMEM((288, 1728), BF16),
            pltpu.VMEM((288, 1152), BF16),
            pltpu.VMEM((288, 864), BF16),
            pltpu.VMEM((96, 192), BF16),
            pltpu.VMEM((192, LANES), F32),
            pltpu.VMEM((96, LANES), F32),
            pltpu.VMEM((96, LANES), F32),
            pltpu.VMEM((96, LANES), F32),
            pltpu.VMEM((6, 6, 96, LANES), F32),
            pltpu.VMEM((6, 4, 96, LANES), F32),
            pltpu.VMEM((2, 6, 96, LANES), BF16),
            pltpu.VMEM((2, 6, 96, LANES), BF16),
            pltpu.VMEM((2, 2, 2, 96, LANES), BF16),
            pltpu.VMEM((2, 2, 2, 96, LANES), BF16),
            pltpu.VMEM((2, 2, 2, 96, LANES), BF16),
            pltpu.VMEM((2, 2, 2, 96, LANES), BF16),
            pltpu.VMEM((4, 384, LANES), F32),
            dma((13,)),
            dma((10,)),
            dma((10,)),
            dma((4,)),
            dma((4,)),
        ],
        compiler_params=pltpu.CompilerParams(
            collective_id=0, has_side_effects=True, vmem_limit_bytes=48 * 1024 * 1024
        ),
        name="residual_block",
    )(
        *(
            pltpu.with_memory_space_constraint(operand, pltpu.HBM)
            for operand in (
                latent.reshape(4, 768, LANES),
                clips,
                gain_in.reshape(1, 192),
                conv_in.reshape(27, 96, 192),
                bias_in.reshape(1, 96),
                gain_mid.reshape(1, 96),
                conv_mid.reshape(27, 96, 96),
                bias_mid.reshape(1, 96),
                skip_weight,
                skip_bias.reshape(1, 96),
            )
        )
    )
    return out.reshape(4, 96, 4, LANES)


def solution(mesh):
    n_t, n_r = mesh.shape["tm"], mesh.shape["rows"]
    return jax.shard_map(
        lambda *args: block(n_t, n_r, *args),
        mesh=mesh,
        in_specs=(P("tm", None, "rows", None),) + (P(),) * 9,
        out_specs=P("tm", None, "rows", None),
        check_vma=False,
    )
```

time: 27.4 us -> 19.9 us (0.73)
  the two profiles are of different devices: /device:TPU:1 before, /device:TPU:27 now
where the time goes in v3:
time: 19.9 us; the launch traced here: 19.8 us
  Pallas kernels  19 us (95%)
  local copies, waits for them, and re-layouts  0.75 us (4%)
    pallas_call x1, Pallas kernels, block(): pl.pallas_call(lambda *refs: body(n_t, n_r, *refs), out_shape=pltpu.VMEM(...  19 us
    unnamed x1, local copies, waits for them, and re-layouts  0.75 us

profile of v3, /device:TPU:27, one launch (start us, length us, event | category | flops | bytes accessed | tf_op | source)
XLA Modules:
  0.0 19.8 jit_solution(1190896192063403895)
XLA Ops:
  0.0 19.0 %residual_block.1 = bf16[4,384,128]{2,1,0:T(8,128)(2,1)S(1)} custom-call(bf16[4,768,128]{2,1,0:T(8,128)(2,1)} %bitcast.11, s32[32]{0:T(128)} %refs_1_.1, f32[1,192]{1,0:T(1,128)} %bitcast.13, bf16[27,96,192]{2,1,0:T(8,128)(2,1)} %bitcast.10, f32[1,96]{1,0:T(1,128)} %bitcast.14, f32[1,96]{1,0:T(1,128)} %bitcast.15, bf16[27,96,96]{2,1,0:T(8,128)(2,1)} %bitcast.12, ...), custom_call_target="tpu_custom_call" | custom-call | tf_op jit(solution)/shard_map/residual_block/pallas_call | solution.py:368
  19.0 0.7 %copy.12 = bf16[4,96,4,128]{3,2,1,0:T(4,128)(2,1)} copy(bf16[4,96,4,128]{3,2,1,0:T(4,128)(2,1)S(1)} %bitcast.9) | data formatting | bytes 786432

commit v4 on v3

v4 whole, which is shorter than its diff:
```python
import jax
import jax.numpy as jnp
from jax import lax
from jax.experimental import pallas as pl
from jax.experimental.pallas import tpu as pltpu
from jax.sharding import PartitionSpec as P

MESH = pl.DeviceIdType.MESH
F32 = jnp.float32
BF16 = jnp.bfloat16
EPS = 1e-6
LANES = 128
PARTS = ((1, 2), (0, 3))


def column(row_ref, scale=1.0):
    size = row_ref.shape[1]
    down = lax.broadcasted_iota(jnp.int32, (size, size), 0)
    across = lax.broadcasted_iota(jnp.int32, (size, size), 1)
    picked = jnp.where(down == across, row_ref[...] * scale, 0.0)
    return jnp.broadcast_to(jnp.sum(picked, axis=1, keepdims=True), (size, LANES))


def norm_silu(values, half_gain):
    mean_sq = jnp.mean(values * values, axis=0, keepdims=True)
    half = values * lax.rsqrt(mean_sq + EPS) * half_gain
    return half + half * jnp.tanh(half)


def put_shifts(x_ref, frame, row, values):
    lane = lax.broadcasted_iota(jnp.int32, values.shape, 1)
    left = jnp.where(lane == 0, 0.0, pltpu.roll(values, 1, 1))
    right = jnp.where(lane == LANES - 1, 0.0, pltpu.roll(values, LANES - 1, 1))
    x_ref[frame, row, 0] = left.astype(BF16)
    x_ref[frame, row, 2] = right.astype(BF16)


class Exchange:
    def __init__(self, copy, sends, gets):
        self.copy, self.sends, self.gets = copy, sends, gets


def body(
    n_t,
    n_r,
    latent_hbm,
    clips_hbm,
    gain_in_hbm,
    conv_in_hbm,
    bias_in_hbm,
    gain_mid_hbm,
    conv_mid_hbm,
    bias_mid_hbm,
    skip_hbm,
    skip_bias_hbm,
    out_ref,
    clips,
    gain_in,
    bias_in,
    gain_mid,
    bias_mid,
    skip_bias,
    latent_v,
    wide,
    raw,
    x1,
    x2,
    taps1,
    taps2,
    w1,
    w1_low,
    w2,
    w2_low,
    w_skip,
    col_in,
    col_bias,
    col_mid,
    col_out,
    acc1,
    acc2,
    edge_out,
    edge_in,
    corner_out1,
    corner_in1,
    corner_out2,
    corner_in2,
    sent1,
    got1,
    sent2,
    got2,
    packed,
    load_sem,
    row_send,
    row_recv,
    time_send,
    time_recv,
):
    t_at = lax.axis_index("tm")
    r_at = lax.axis_index("rows")
    has_up, has_down = r_at > 0, r_at < n_r - 1
    up, down = {"rows": r_at - 1}, {"rows": r_at + 1}
    before, after = {"tm": lax.rem(t_at + n_t - 1, n_t)}, {"tm": lax.rem(t_at + 1, n_t)}

    barrier = pltpu.get_barrier_semaphore()
    def greet(*peers):
        for peer in peers:
            pl.semaphore_signal(barrier, inc=1, device_id=peer, device_id_type=MESH)

    greet(before)
    pl.when(has_up)(lambda: greet(up, before | up))
    pl.when(has_down)(lambda: greet(down, before | down))

    def load(src, dst, slot):
        return pltpu.make_async_copy(src, dst, load_sem.at[slot])

    load_gain = load(gain_in_hbm, gain_in, 0)
    load_latent = {f: load(latent_hbm.at[f], latent_v.at[f], 1 + f) for f in (2, 3, 0, 1)}
    load_taps = {i: load(conv_in_hbm.at[:, i], taps1.at[:, i], 5 + i) for i in (0, 2, 1)}
    load_clips = load(clips_hbm, clips, 8)
    load_bias = load(bias_in_hbm, bias_in, 9)
    load_mid = [load(gain_mid_hbm, gain_mid, 10), load(bias_mid_hbm, bias_mid, 11), load(skip_bias_hbm, skip_bias, 12)]
    load_mid += [load(skip_hbm, w_skip, 13), load(conv_mid_hbm, taps2, 14)]
    first_loads = [load_gain, load_clips, load_latent[2], load_latent[3], load_taps[0], load_taps[2]]
    first_loads += [load_latent[0], load_latent[1]]
    late_loads = [load_taps[1], load_bias] + load_mid
    for copy in first_loads + late_loads:
        copy.start()

    def clear(ref, *at):
        part = ref.at[at] if at else ref
        part[...] = jnp.zeros(part.shape, BF16)

    @pl.when(jnp.logical_not(has_up))
    def _():
        clear(edge_in, 1)
        clear(corner_in1, 1)
        clear(corner_in2, 1)
        for f in range(4):
            clear(x2, f, 0)

    @pl.when(jnp.logical_not(has_down))
    def _():
        clear(edge_in, 0)
        clear(corner_in1, 0)
        clear(corner_in2, 0)
        for f in range(4):
            clear(x2, f, 5)

    def remote(src, dst, sems, slot, peer, sends=None, gets=None):
        copy = pltpu.make_async_remote_copy(
            src_ref=src,
            dst_ref=dst,
            send_sem=sems[0].at[slot],
            recv_sem=sems[1].at[slot],
            device_id=peer,
            device_id_type=MESH,
        )
        return copy if sends is None else Exchange(copy, sends, gets)

    row_sems, time_sems = (row_send, row_recv), (time_send, time_recv)
    sides = ((up, has_up, has_down), (down, has_down, has_up))

    def by_row(src_of, dst_of, slot):
        return [remote(src_of(k), dst_of(k), row_sems, slot + k, *side) for k, side in enumerate(sides)]

    def by_corner(src, dst, slot):
        return [
            remote(src.at[k], dst.at[k], row_sems, slot + k, after | peer, sends, gets)
            for k, (peer, sends, gets) in enumerate(sides)
        ]

    def by_time(src, dst, slot):
        return [
            remote(src.at[part], dst.at[part], time_sems, slot + part, after) for part in range(2)
        ]

    rows1 = {g: by_row(lambda k: edge_out.at[k, pl.ds(g, 2)], lambda k: edge_in.at[k, pl.ds(g, 2)], g) for g in (2, 0)}
    rows2 = {
        f: by_row(lambda k: x2.at[pl.ds(f, 2), (1, 4)[k], 1], lambda k: x2.at[pl.ds(f, 2), (5, 0)[k], 1], 4 + f)
        for f in (2, 0)
    }
    corners1 = by_corner(corner_out1, corner_in1, 8)
    corners2 = by_corner(corner_out2, corner_in2, 10)
    times1 = by_time(sent1, got1, 0)
    times2 = by_time(sent2, got2, 2)

    def start(*exchanges):
        for sides_of in zip(*exchanges):

            @pl.when(sides_of[0].sends)
            def _(sides_of=sides_of):
                for exchange in sides_of:
                    exchange.copy.start()

    def arrived(*exchanges):
        for sides_of in zip(*exchanges):

            @pl.when(sides_of[0].gets)
            def _(sides_of=sides_of):
                for exchange in sides_of:
                    exchange.copy.wait_recv()

    def left(*exchanges):
        for sides_of in zip(*exchanges):

            @pl.when(sides_of[0].sends)
            def _(sides_of=sides_of):
                for exchange in sides_of:
                    exchange.copy.wait_send()

    def spread(frame):
        wide[frame] = latent_v[frame].astype(F32)

    def first_act(frame, rows):
        for row in rows:
            values = wide[frame, pl.ds(row, 192, stride=4), :]
            raw[frame, row] = values.astype(BF16)
            act = norm_silu(values, col_in[...])
            x1[frame, row, 1] = act.astype(BF16)
            put_shifts(x1, frame, row, act)

    seen = set()

    def gather(acc, first, row, terms, taps, base, keeps_target):
        sums = {}
        for k, f in enumerate((first, first + 1)):
            for n, tap in enumerate(taps):
                target = f + 2 - tap
                if not keeps_target(target):
                    continue
                value = terms[n * 96 : (n + 1) * 96, k * LANES : (k + 1) * LANES]
                if target > f:
                    value = value * keeps[target, target - f]
                sums[target] = value if target not in sums else sums[target] + value
        for target, value in sums.items():
            key = (id(acc), target, row)
            if key in seen:
                value = value + acc[target, row]
            elif base is not None and target < 4 and 1 <= row <= 4:
                value = value + base
            seen.add(key)
            acc[target, row] = value

    sources = {-1: (0,), 0: (1, 0), 1: (0, 1, 2), 2: (1, 2, 3), 3: (2, 3), 4: (3,)}

    def conv1(first, targets):
        for target in targets:
            rows = sources[target]
            slab = jnp.concatenate(
                [jnp.concatenate([x1[f, row].reshape(576, LANES) for row in rows], axis=0) for f in (first, first + 1)],
                axis=1,
            )
            weight = (w1_low if target < 1 else w1)[:, : 576 * len(rows)]
            terms = jnp.dot(weight, slab, preferred_element_type=F32)
            gather(acc1, first, target + 1, terms, (0, 1, 2), col_bias[...] if 0 <= target < 4 else None, lambda g: True)

    def conv2_part(first, target, rows, weight, taps, keeps_target):
        slab = jnp.concatenate(
            [jnp.concatenate([x2[f, row + 1].reshape(288, LANES) for row in rows], axis=0) for f in (first, first + 1)],
            axis=1,
        )
        weight = weight[pl.ds(96 * taps[0], 96 * len(taps)), : 288 * len(rows)]
        terms = jnp.dot(weight, slab, preferred_element_type=F32)
        gather(acc2, first, target + 1, terms, taps, None, keeps_target)

    def conv2(first, targets):
        for target in targets:
            weight = w2_low if target < 1 else w2
            if target in (-1, 4):
                conv2_part(first, target, sources[target], weight, (0, 1), lambda g: g >= 4)
            else:
                conv2_part(first, target, sources[target], weight, (0, 1, 2), lambda g: True)

    def halo2(first):
        for row in (0, 5):
            for frame in (first, first + 1):
                put_shifts(x2, frame, row, x2[frame, row, 1].astype(F32))
        taps = (1, 2) if first == 2 else (0, 1, 2)
        conv2_part(first, 0, (-1,), w2, taps, lambda g: g < 4)
        conv2_part(first, 3, (4,), w2_low, taps, lambda g: g < 4)

    def edges_out(g):
        for k, row in enumerate((0, 5)):
            for frame in (g, g + 1):
                edge_out[k, frame] = acc1[frame, row].astype(BF16)

    def corners_out(acc, buf):
        for k, row in enumerate((0, 5)):
            for g in range(2):
                buf[k, g] = acc[4 + g, row].astype(BF16)

    def pass_on(acc, buf, copies, part):
        for g in range(2):
            for k, row in enumerate(PARTS[part]):
                buf[part, g, k] = acc[4 + g, row + 1].astype(BF16)
        copies[part].start()

    def with_time(values, frame, row, got, corner):
        if frame < 2:
            part = 1 if row in (0, 3) else 0
            values = values + got[part, frame, PARTS[part].index(row)].astype(F32)
            if part:
                values = values + corner[1 if row == 0 else 0, frame].astype(F32)
        return values

    def second_act(frame, part, shifted=True):
        for row in PARTS[part]:
            values = acc1[frame, row + 1]
            if part:
                values = values + edge_in[1 if row == 0 else 0, frame].astype(F32)
            values = with_time(values, frame, row, got1, corner_in1)
            act = norm_silu(values, col_mid[...])
            x2[frame, row + 1, 1] = act.astype(BF16)
            if shifted:
                put_shifts(x2, frame, row + 1, act)

    def shift_edges(first):
        for frame in (first, first + 1):
            for row in (1, 4):
                put_shifts(x2, frame, row, x2[frame, row, 1].astype(F32))

    def shortcut(row):
        slab = jnp.concatenate([raw[f, row] for f in range(4)], axis=1)
        terms = jnp.dot(w_skip[...], slab, preferred_element_type=F32)
        for f in range(4):
            acc2[f, row + 1] = terms[:, f * LANES : (f + 1) * LANES] + col_out[...]
            seen.add((id(acc2), f, row + 1))

    def finish(frame, part):
        for row in PARTS[part]:
            packed[frame, pl.ds(row, 96, stride=4), :] = with_time(acc2[frame, row + 1], frame, row, got2, corner_in2)

    def pack(dst, src, block, row_tap, size):
        for tap in range(3):
            dst[pl.ds(tap * 96, 96), pl.ds(block * 3 * size, 3 * size)] = jnp.concatenate(
                [src[tap, row_tap, k] for k in range(3)], axis=1
            )

    load_gain.wait()
    col_in[...] = column(gain_in, 0.5)
    load_clips.wait()
    total = clips.shape[0]

    def keep(frame, back):
        at = t_at * 4 + frame
        own = clips[jnp.minimum(at, total - 1)]
        past = clips[jnp.clip(at - back, 0, total - 1)]
        good = (own == past) & (at < total) & (at >= back)
        return jnp.where(good, 1.0, 0.0).astype(F32)

    keeps = {(f, d): keep(f, d) for f in range(1, 6) for d in (1, 2) if 0 <= f - d < 4}
    for copy in first_loads[2:]:
        copy.wait()
    pack(w1, taps1, 0, 0, 192)
    pack(w1_low, taps1, 0, 2, 192)
    for frame in (2, 3, 0, 1):
        spread(frame)
        first_act(frame, (0, 3))
    conv1(2, (-1, 4))
    conv1(0, (-1, 4))
    edges_out(2)
    edges_out(0)
    corners_out(acc1, corner_out1)
    greeted = 1 + 2 * has_up.astype(jnp.int32) + 2 * has_down.astype(jnp.int32)
    pl.semaphore_wait(barrier, greeted)
    start(rows1[2], corners1, rows1[0])
    load_taps[1].wait()
    load_bias.wait()
    col_bias[...] = column(bias_in)
    for tap in range(3):
        rest = [taps1[tap, i, k] for i in (0, 1, 2) for k in range(3)]
        w1[pl.ds(tap * 96, 96), :] = jnp.concatenate(rest, axis=1)
        w1_low[pl.ds(tap * 96, 96), :] = jnp.concatenate(rest[6:] + rest[3:6], axis=1)
    for frame in (2, 3):
        first_act(frame, (1, 2))
    conv1(2, (0, 3))
    pass_on(acc1, sent1, times1, 1)
    conv1(2, (1, 2))
    pass_on(acc1, sent1, times1, 0)
    for frame in (0, 1):
        first_act(frame, (1, 2))
    conv1(0, (0, 3, 1, 2))
    for copy in load_mid:
        copy.wait()
    col_mid[...] = column(gain_mid, 0.5)
    col_out[...] = column(bias_mid) + column(skip_bias)
    for tap in range(3):
        rest = [taps2[tap, i, k] for i in (0, 1, 2) for k in range(3)]
        w2[pl.ds(tap * 96, 96), :] = jnp.concatenate(rest, axis=1)
        w2_low[pl.ds(tap * 96, 96), :] = jnp.concatenate(rest[6:] + rest[3:6], axis=1)
    for frame in (2, 3):
        second_act(frame, 0)
    for row in range(4):
        shortcut(row)
    arrived(rows1[2])
    for frame in (2, 3):
        second_act(frame, 1, shifted=False)
    start(rows2[2])
    shift_edges(2)
    conv2(2, (-1, 4))
    corners_out(acc2, corner_out2)
    start(corners2)
    conv2(2, (0, 3))
    pass_on(acc2, sent2, times2, 1)
    arrived(rows1[0], corners1)
    times1[1].wait_recv()
    for frame in (0, 1):
        second_act(frame, 1, shifted=False)
    start(rows2[0])
    shift_edges(0)
    conv2(2, (1, 2))
    pass_on(acc2, sent2, times2, 0)
    times1[0].wait_recv()
    for frame in (0, 1):
        second_act(frame, 0)
    conv2(0, (0, 3, 1, 2))
    arrived(rows2[2])
    halo2(2)
    for frame in (2, 3):
        finish(frame, 0)
    times2[0].wait_recv()
    times2[1].wait_recv()
    arrived(corners2, rows2[0])
    for frame in (0, 1):
        finish(frame, 0)
    halo2(0)
    for frame in range(4):
        finish(frame, 1)
        out_ref[frame] = packed[frame].astype(BF16)
    left(rows1[2], rows1[0], rows2[2], rows2[0], corners1, corners2)
    for copy in times1 + times2:
        copy.wait_send()


def block(n_t, n_r, latent, clips, gain_in, conv_in, bias_in, gain_mid, conv_mid, bias_mid, skip_weight, skip_bias):
    hbm = pl.BlockSpec(memory_space=pltpu.HBM)
    dma = pltpu.SemaphoreType.DMA
    out = pl.pallas_call(
        lambda *refs: body(n_t, n_r, *refs),
        out_shape=pltpu.VMEM((4, 384, LANES), BF16),
        in_specs=[hbm] * 10,
        out_specs=pl.BlockSpec(memory_space=pltpu.VMEM),
        scratch_shapes=[
            pltpu.SMEM(clips.shape, jnp.int32),
            pltpu.VMEM((1, 192), F32),
            pltpu.VMEM((1, 96), F32),
            pltpu.VMEM((1, 96), F32),
            pltpu.VMEM((1, 96), F32),
            pltpu.VMEM((1, 96), F32),
            pltpu.VMEM((4, 768, LANES), BF16),
            pltpu.VMEM((4, 768, LANES), F32),
            pltpu.VMEM((4, 4, 192, LANES), BF16),
            pltpu.VMEM((4, 4, 3, 192, LANES), BF16),
            pltpu.VMEM((4, 6, 3, 96, LANES), BF16),
            pltpu.VMEM((3, 3, 3, 96, 192), BF16),
            pltpu.VMEM((3, 3, 3, 96, 96), BF16),
            pltpu.VMEM((288, 1728), BF16),
            pltpu.VMEM((288, 1152), BF16),
            pltpu.VMEM((288, 864), BF16),
            pltpu.VMEM((288, 576), BF16),
            pltpu.VMEM((96, 192), BF16),
            pltpu.VMEM((192, LANES), F32),
            pltpu.VMEM((96, LANES), F32),
            pltpu.VMEM((96, LANES), F32),
            pltpu.VMEM((96, LANES), F32),
            pltpu.VMEM((6, 6, 96, LANES), F32),
            pltpu.VMEM((6, 6, 96, LANES), F32),
            pltpu.VMEM((2, 4, 96, LANES), BF16),
            pltpu.VMEM((2, 4, 96, LANES), BF16),
            pltpu.VMEM((2, 2, 96, LANES), BF16),
            pltpu.VMEM((2, 2, 96, LANES), BF16),
            pltpu.VMEM((2, 2, 96, LANES), BF16),
            pltpu.VMEM((2, 2, 96, LANES), BF16),
            pltpu.VMEM((2, 2, 2, 96, LANES), BF16),
            pltpu.VMEM((2, 2, 2, 96, LANES), BF16),
            pltpu.VMEM((2, 2, 2, 96, LANES), BF16),
            pltpu.VMEM((2, 2, 2, 96, LANES), BF16),
            pltpu.VMEM((4, 384, LANES), F32),
            dma((15,)),
            dma((12,)),
            dma((12,)),
            dma((4,)),
            dma((4,)),
        ],
        compiler_params=pltpu.CompilerParams(
            collective_id=0, has_side_effects=True, vmem_limit_bytes=48 * 1024 * 1024
        ),
        name="residual_block",
    )(
        *(
            pltpu.with_memory_space_constraint(operand, pltpu.HBM)
            for operand in (
                latent.reshape(4, 768, LANES),
                clips,
                gain_in.reshape(1, 192),
                conv_in,
                bias_in.reshape(1, 96),
                gain_mid.reshape(1, 96),
                conv_mid,
                bias_mid.reshape(1, 96),
                skip_weight,
                skip_bias.reshape(1, 96),
            )
        )
    )
    return out.reshape(4, 96, 4, LANES)


def solution(mesh):
    n_t, n_r = mesh.shape["tm"], mesh.shape["rows"]
    return jax.shard_map(
        lambda *args: block(n_t, n_r, *args),
        mesh=mesh,
        in_specs=(P("tm", None, "rows", None),) + (P(),) * 9,
        out_specs=P("tm", None, "rows", None),
        check_vma=False,
    )
```

time: 19.9 us -> 19.2 us (0.965)
  Pallas kernels: 19 us -> 18.3 us
    pallas_call x1, Pallas kernels: 19 us -> 18.3 us  [block(): pl.pallas_call(lambda *refs: body(n_t, n_r, *refs), out_shape=pltpu.VMEM(...]
where the time goes in v4:
time: 19.2 us; the launch traced here: 19.1 us
  Pallas kernels  18.3 us (95%)
  local copies, waits for them, and re-layouts  0.75 us (4%)
    pallas_call x1, Pallas kernels, block(): pl.pallas_call(lambda *refs: body(n_t, n_r, *refs), out_shape=pltpu.VMEM(...  18.3 us
    unnamed x1, local copies, waits for them, and re-layouts  0.75 us

profile of v4, /device:TPU:27, one launch (start us, length us, event | category | flops | bytes accessed | tf_op | source)
XLA Modules:
  0.0 19.1 jit_solution(13590191230600810084)
XLA Ops:
  0.0 18.3 %residual_block.1 = bf16[4,384,128]{2,1,0:T(8,128)(2,1)S(1)} custom-call(bf16[4,768,128]{2,1,0:T(8,128)(2,1)} %bitcast.8, s32[32]{0:T(128)} %refs_1_.1, f32[1,192]{1,0:T(1,128)} %bitcast.9, bf16[3,3,3,96,192]{4,3,2,1,0:T(8,128)(2,1)} %refs_3_.1, f32[1,96]{1,0:T(1,128)} %bitcast.10, f32[1,96]{1,0:T(1,128)} %bitcast.11, bf16[3,3,3,96,96]{4,3,2,1,0:T(8,128)(2,1)} %refs_6_.1, ...), custom_call_target="tpu_custom_call" | custom-call | tf_op jit(solution)/shard_map/residual_block/pallas_call | solution.py:438
  18.3 0.7 %copy.12 = bf16[4,96,4,128]{3,2,1,0:T(4,128)(2,1)} copy(bf16[4,96,4,128]{3,2,1,0:T(4,128)(2,1)S(1)} %bitcast.7) | data formatting | bytes 786432

commit v5 on v4

--- a/solution.py
+++ b/solution.py
@@ -99,16 +99,19 @@
     r_at = lax.axis_index("rows")
     has_up, has_down = r_at > 0, r_at < n_r - 1
     up, down = {"rows": r_at - 1}, {"rows": r_at + 1}
-    before, after = {"tm": lax.rem(t_at + n_t - 1, n_t)}, {"tm": lax.rem(t_at + 1, n_t)}
+    has_before, has_after = t_at > 0, t_at < n_t - 1
+    before, after = {"tm": t_at - 1}, {"tm": t_at + 1}
 
     barrier = pltpu.get_barrier_semaphore()
     def greet(*peers):
         for peer in peers:
             pl.semaphore_signal(barrier, inc=1, device_id=peer, device_id_type=MESH)
 
-    greet(before)
-    pl.when(has_up)(lambda: greet(up, before | up))
-    pl.when(has_down)(lambda: greet(down, before | down))
+    pl.when(has_before)(lambda: greet(before))
+    pl.when(has_up)(lambda: greet(up))
+    pl.when(has_down)(lambda: greet(down))
+    pl.when(has_before & has_up)(lambda: greet(before | up))
+    pl.when(has_before & has_down)(lambda: greet(before | down))
 
     def load(src, dst, slot):
         return pltpu.make_async_copy(src, dst, load_sem.at[slot])
@@ -133,20 +136,31 @@
     @pl.when(jnp.logical_not(has_up))
     def _():
         clear(edge_in, 1)
-        clear(corner_in1, 1)
-        clear(corner_in2, 1)
         for f in range(4):
             clear(x2, f, 0)
 
     @pl.when(jnp.logical_not(has_down))
     def _():
         clear(edge_in, 0)
+        for f in range(4):
+            clear(x2, f, 5)
+
+    @pl.when(jnp.logical_not(has_before))
+    def _():
+        clear(got1)
+        clear(got2)
+
+    @pl.when(jnp.logical_not(has_before & has_up))
+    def _():
+        clear(corner_in1, 1)
+        clear(corner_in2, 1)
+
+    @pl.when(jnp.logical_not(has_before & has_down))
+    def _():
         clear(corner_in1, 0)
         clear(corner_in2, 0)
-        for f in range(4):
-            clear(x2, f, 5)
-
-    def remote(src, dst, sems, slot, peer, sends=None, gets=None):
+
+    def remote(src, dst, sems, slot, peer, sends, gets):
         copy = pltpu.make_async_remote_copy(
             src_ref=src,
             dst_ref=dst,
@@ -155,7 +169,7 @@
             device_id=peer,
             device_id_type=MESH,
         )
-        return copy if sends is None else Exchange(copy, sends, gets)
+        return Exchange(copy, sends, gets)
 
     row_sems, time_sems = (row_send, row_recv), (time_send, time_recv)
     sides = ((up, has_up, has_down), (down, has_down, has_up))
@@ -165,13 +179,14 @@
 
     def by_corner(src, dst, slot):
         return [
-            remote(src.at[k], dst.at[k], row_sems, slot + k, after | peer, sends, gets)
+            remote(src.at[k], dst.at[k], row_sems, slot + k, after | peer, sends & has_after, gets & has_before)
             for k, (peer, sends, gets) in enumerate(sides)
         ]
 
     def by_time(src, dst, slot):
         return [
-            remote(src.at[part], dst.at[part], time_sems, slot + part, after) for part in range(2)
+            [remote(src.at[part], dst.at[part], time_sems, slot + part, after, has_after, has_before)]
+            for part in range(2)
         ]
 
     rows1 = {g: by_row(lambda k: edge_out.at[k, pl.ds(g, 2)], lambda k: edge_in.at[k, pl.ds(g, 2)], g) for g in (2, 0)}
@@ -293,7 +308,7 @@
         for g in range(2):
             for k, row in enumerate(PARTS[part]):
                 buf[part, g, k] = acc[4 + g, row + 1].astype(BF16)
-        copies[part].start()
+        start(copies[part])
 
     def with_time(values, frame, row, got, corner):
         if frame < 2:
@@ -361,16 +376,21 @@
     edges_out(2)
     edges_out(0)
     corners_out(acc1, corner_out1)
-    greeted = 1 + 2 * has_up.astype(jnp.int32) + 2 * has_down.astype(jnp.int32)
+    friends = (has_up, has_down, has_after, has_after & has_up, has_after & has_down)
+    greeted = sum(there.astype(jnp.int32) for there in friends)
     pl.semaphore_wait(barrier, greeted)
-    start(rows1[2], corners1, rows1[0])
+    start(rows1[2])
+    start(corners1)
+    start(rows1[0])
     load_taps[1].wait()
     load_bias.wait()
     col_bias[...] = column(bias_in)
     for tap in range(3):
-        rest = [taps1[tap, i, k] for i in (0, 1, 2) for k in range(3)]
-        w1[pl.ds(tap * 96, 96), :] = jnp.concatenate(rest, axis=1)
-        w1_low[pl.ds(tap * 96, 96), :] = jnp.concatenate(rest[6:] + rest[3:6], axis=1)
+        at = pl.ds(tap * 96, 96)
+        middle = [taps1[tap, 1, k] for k in range(3)]
+        last = [taps1[tap, 2, k] for k in range(3)]
+        w1[at, pl.ds(512, 1216)] = jnp.concatenate([w1[at, pl.ds(512, 64)]] + middle + last, axis=1)
+        w1_low[at, pl.ds(512, 640)] = jnp.concatenate([w1_low[at, pl.ds(512, 64)]] + middle, axis=1)
     for frame in (2, 3):
         first_act(frame, (1, 2))
     conv1(2, (0, 3))
@@ -397,20 +417,21 @@
         second_act(frame, 1, shifted=False)
     start(rows2[2])
     shift_edges(2)
+    conv2(2, (0, 3))
+    pass_on(acc2, sent2, times2, 1)
     conv2(2, (-1, 4))
     corners_out(acc2, corner_out2)
     start(corners2)
-    conv2(2, (0, 3))
-    pass_on(acc2, sent2, times2, 1)
-    arrived(rows1[0], corners1)
-    times1[1].wait_recv()
+    arrived(rows1[0])
+    arrived(corners1)
+    arrived(times1[1])
     for frame in (0, 1):
         second_act(frame, 1, shifted=False)
     start(rows2[0])
     shift_edges(0)
     conv2(2, (1, 2))
     pass_on(acc2, sent2, times2, 0)
-    times1[0].wait_recv()
+    arrived(times1[0])
     for frame in (0, 1):
         second_act(frame, 0)
     conv2(0, (0, 3, 1, 2))
@@ -418,18 +439,18 @@
     halo2(2)
     for frame in (2, 3):
         finish(frame, 0)
-    times2[0].wait_recv()
-    times2[1].wait_recv()
-    arrived(corners2, rows2[0])
+    arrived(times2[0], times2[1])
+    arrived(corners2)
+    arrived(rows2[0])
     for frame in (0, 1):
         finish(frame, 0)
     halo2(0)
     for frame in range(4):
         finish(frame, 1)
         out_ref[frame] = packed[frame].astype(BF16)
-    left(rows1[2], rows1[0], rows2[2], rows2[0], corners1, corners2)
-    for copy in times1 + times2:
-        copy.wait_send()
+    left(rows1[2], rows1[0], rows2[2], rows2[0])
+    left(corners1, corners2)
+    left(*times1, *times2)
 
 
 def block(n_t, n_r, latent, clips, gain_in, conv_in, bias_in, gain_mid, conv_mid, bias_mid, skip_weight, skip_bias):

time: 19.2 us -> 19.2 us (level)
  no operation moved by 1% of the time
where the time goes in v5:
time: 19.2 us; the launch traced here: 19.1 us
  Pallas kernels  18.3 us (95%)
  local copies, waits for them, and re-layouts  0.75 us (4%)
    pallas_call x1, Pallas kernels, block(): pl.pallas_call(lambda *refs: body(n_t, n_r, *refs), out_shape=pltpu.VMEM(...  18.3 us
    unnamed x1, local copies, waits for them, and re-layouts  0.75 us

profile of v5, /device:TPU:27, one launch (start us, length us, event | category | flops | bytes accessed | tf_op | source)
XLA Modules:
  0.0 19.1 jit_solution(1865736566789340769)
XLA Ops:
  0.0 18.3 %residual_block.1 = bf16[4,384,128]{2,1,0:T(8,128)(2,1)S(1)} custom-call(bf16[4,768,128]{2,1,0:T(8,128)(2,1)} %bitcast.8, s32[32]{0:T(128)} %refs_1_.1, f32[1,192]{1,0:T(1,128)} %bitcast.9, bf16[3,3,3,96,192]{4,3,2,1,0:T(8,128)(2,1)} %refs_3_.1, f32[1,96]{1,0:T(1,128)} %bitcast.10, f32[1,96]{1,0:T(1,128)} %bitcast.11, bf16[3,3,3,96,96]{4,3,2,1,0:T(8,128)(2,1)} %refs_6_.1, ...), custom_call_target="tpu_custom_call" | custom-call | tf_op jit(solution)/shard_map/residual_block/pallas_call | solution.py:459
  18.3 0.7 %copy.12 = bf16[4,96,4,128]{3,2,1,0:T(4,128)(2,1)} copy(bf16[4,96,4,128]{3,2,1,0:T(4,128)(2,1)S(1)} %bitcast.7) | data formatting | bytes 786432
